TPU v7x, 128 devices: a whole 4x4x4 slice. The times are simulated.
128 devices in a mesh: req: 32 (over y, z, core), tp: 4 (over x).
Axes of the slice: x: 4, y: 4, z: 4, core: 2. Of those that a mesh axis runs over, the one named last changes fastest.
Arguments:
- tokens: bfloat16 [512, 2048], P('req'), may hold values from -6 to 6
- lengths: int32 [512], P('req'), may hold values from 1 to 8192, 131072 in all
- pool_order: int32 [512], replicated, may hold values from 0 to 511, each once
- positions: int32 [512], P('req'), may hold values from 0 to 16383
- slot_mask: int32 [131072], P('req'), may hold values 0 or 1
- kv_cache: bfloat16 [131072, 2, 1024], P('req', None, 'tp'), may hold values from -420 to 420
- attn_gain: bfloat16 [2048], replicated, may hold values from 0.25 to 1.75
- w_query: bfloat16 [2048, 2048], P(None, 'tp'), may hold values from -0.125 to 0.125
- w_key: bfloat16 [2048, 1024], P(None, 'tp'), may hold values from -0.125 to 0.125
- w_value: bfloat16 [2048, 1024], P(None, 'tp'), may hold values from -0.125 to 0.125
- w_out: bfloat16 [2048, 2048], P('tp'), may hold values from -0.125 to 0.125
- ffn_gain: bfloat16 [2048], replicated, may hold values from 0.25 to 1.75
- w_gate: bfloat16 [2048, 4096], P(None, 'tp'), may hold values from -0.125 to 0.125
- w_up: bfloat16 [2048, 4096], P(None, 'tp'), may hold values from -0.125 to 0.125
- w_down: bfloat16 [4096, 2048], P('tp'), may hold values from -0.09375 to 0.09375
Outputs:
- hidden_out: float32 [512, 2048], P('req')
- new_kv: float32 [512, 2, 1024], P('req', None, 'tp')
Inputs may be any that keep to these rules, and one draw needn't show every extreme that they name: The lengths add up to 131072, so the requests' caches fill the pool end to end; the largest is exactly 8192. `pool_order`: each request appears exactly once.
All inputs are finite; a program needn't handle non-finite values. No bound on the sum of `lengths` or of `slot_mask` on one device may be relied on, other than what follows from the above.
Results may differ from a plain program's by a relative error of at most 0.013.
The roundings to bfloat16 on the way count: a program that leaves them out, or rounds other values in their place, can miss the bound.
Values may be sent and summed in bfloat16 or wider, within the bound.
A program may use at most 192 MiB of HBM per device.

v0:
```python
import math

import jax
import jax.numpy as jnp
from jax import lax
from jax.sharding import PartitionSpec as P

HEAD_DIM = 128


ROPE_BASE = 1000000.0
EPS = 1e-05
FLOOR = -1e30


def joined(part, axis, combine):
    gathered = jax.tree.map(lambda a: lax.all_gather(a, axis), part)

    def take(source):
        return jax.tree.map(lambda a: lax.dynamic_index_in_dim(a, source, 0, False), gathered)

    return lax.fori_loop(
        1, lax.axis_size(axis), lambda source, state: combine(state, take(source)), take(0)
    )


def rms_norm(rows, gain):
    mean_sq = jnp.mean(rows * rows, axis=-1, keepdims=True)
    return rows * lax.rsqrt(mean_sq + EPS) * gain.astype(jnp.float32)


def rotate(vectors, places):
    width = vectors.shape[-1]
    half = width // 2
    freq = ROPE_BASE ** (-(jnp.arange(half, dtype=jnp.float32) * 2.0) / width)
    angle = places.astype(jnp.float32)[:, None] * freq[None, :]
    cosine = jnp.cos(angle)[:, None, :]
    sine = jnp.sin(angle)[:, None, :]
    first = vectors[..., :half]
    second = vectors[..., half:]
    return jnp.concatenate(
        [first * cosine - second * sine, second * cosine + first * sine], axis=-1
    )


def combine_parts(first, second):
    peak = jnp.maximum(first[0], second[0])
    left = jnp.exp(first[0] - peak)
    right = jnp.exp(second[0] - peak)
    return (
        peak,
        first[1] * left + second[1] * right,
        first[2] * left[..., None] + second[2] * right[..., None],
    )


def per_device(
    tokens,
    lengths,
    pool_order,
    positions,
    slot_mask,
    kv_cache,
    attn_gain,
    w_query,
    w_key,
    w_value,
    w_out,
    ffn_gain,
    w_gate,
    w_up,
    w_down,
):
    count = tokens.shape[0]
    head_dim = HEAD_DIM
    kv_local = w_key.shape[1] // head_dim
    q_local = w_query.shape[1] // head_dim
    group = q_local // kv_local
    slot_count = kv_cache.shape[0]
    scale = 1.0 / math.sqrt(head_dim)
    highest = lax.Precision.HIGHEST
    all_lengths = lax.all_gather(lengths, "req", axis=0, tiled=True)
    total_reqs = all_lengths.shape[0]
    ordered = all_lengths[pool_order]
    ends = jnp.cumsum(ordered)
    base = lax.axis_index("req") * slot_count
    slot_ids = base + jnp.arange(slot_count, dtype=jnp.int32)
    place = jnp.searchsorted(ends, slot_ids, side="right")
    owner = pool_order[place]
    belongs = owner[:, None] == jnp.arange(total_reqs, dtype=jnp.int32)[None, :]
    belongs_f = belongs.astype(jnp.float32)
    rows = tokens.astype(jnp.float32)
    normed = rms_norm(rows, attn_gain).astype(jnp.bfloat16)
    query = rotate(
        jnp.dot(normed, w_query, preferred_element_type=jnp.float32).reshape(
            count, q_local, head_dim
        ),
        positions,
    ).astype(jnp.bfloat16)
    key_full = rotate(
        jnp.dot(normed, w_key, preferred_element_type=jnp.float32).reshape(
            count, kv_local, head_dim
        ),
        positions,
    )
    value_full = jnp.dot(normed, w_value, preferred_element_type=jnp.float32)
    new_kv = jnp.stack([key_full.reshape(count, kv_local * head_dim), value_full], axis=1)
    new_key = key_full.astype(jnp.bfloat16)
    new_value = value_full.astype(jnp.bfloat16)
    everyone = lax.all_gather(query.reshape(count, q_local * head_dim), "req", axis=0, tiled=True)
    picked = everyone[owner].reshape(slot_count, kv_local, group, head_dim)
    keys = kv_cache[:, 0, :].reshape(slot_count, kv_local, head_dim)
    values = kv_cache[:, 1, :].reshape(slot_count, kv_local, head_dim)
    scores = jnp.einsum("skgd,skd->skg", picked, keys, preferred_element_type=jnp.float32) * scale
    live = (slot_mask == 1)[:, None, None]
    scores = jnp.where(live, scores, FLOOR)
    peak_heads = []
    for head in range(kv_local):
        masked = jnp.where(belongs[:, :, None], scores[:, head, :][:, None, :], FLOOR)
        peak_heads.append(jnp.max(masked, axis=0))
    peak = jnp.stack(peak_heads, axis=1)
    weights = jnp.where(live, jnp.exp(scores - peak[owner]), 0.0)
    total = jnp.dot(
        belongs_f.T,
        weights.reshape(slot_count, kv_local * group),
        precision=highest,
        preferred_element_type=jnp.float32,
    ).reshape(total_reqs, kv_local, group)
    sum_heads = []
    for head in range(kv_local):
        spread = belongs_f[:, :, None] * weights[:, head, :][:, None, :]
        head_values = values[:, head, :].astype(jnp.float32)
        sum_heads.append(
            jnp.einsum(
                "srg,sd->rgd",
                spread,
                head_values,
                precision=highest,
                preferred_element_type=jnp.float32,
            )
        )
    summed = jnp.stack(sum_heads, axis=1)
    start = lax.axis_index("req") * count
    merged = joined((peak, total, summed), "req", combine_parts)
    own_peak = lax.dynamic_slice_in_dim(merged[0], start, count, 0)
    own_total = lax.dynamic_slice_in_dim(merged[1], start, count, 0)
    own_sum = lax.dynamic_slice_in_dim(merged[2], start, count, 0)
    own_query = query.reshape(count, kv_local, group, head_dim)
    own_score = (
        jnp.einsum("nkgd,nkd->nkg", own_query, new_key, preferred_element_type=jnp.float32) * scale
    )
    final_peak = jnp.maximum(own_peak, own_score)
    old_part = jnp.exp(own_peak - final_peak)
    new_part = jnp.exp(own_score - final_peak)
    denom = own_total * old_part + new_part
    numer = own_sum * old_part[..., None] + new_part[..., None] * new_value.reshape(
        count, kv_local, 1, head_dim
    ).astype(jnp.float32)
    context = (numer / denom[..., None]).reshape(count, q_local * head_dim).astype(jnp.bfloat16)
    partial_attn = jnp.dot(context, w_out, preferred_element_type=jnp.float32)
    mid = rows + lax.psum(partial_attn, "tp")
    normed_mid = rms_norm(mid, ffn_gain).astype(jnp.bfloat16)
    gate = jnp.dot(normed_mid, w_gate, preferred_element_type=jnp.float32)
    upper = jnp.dot(normed_mid, w_up, preferred_element_type=jnp.float32)
    act = (jax.nn.silu(gate) * upper).astype(jnp.bfloat16)
    down_part = jnp.dot(act, w_down, preferred_element_type=jnp.float32)
    hidden_out = mid + lax.psum(down_part, "tp")
    return (hidden_out, new_kv)


def solution(mesh):
    placed = (
        P("req", None),
        P("req"),
        P(),
        P("req"),
        P("req"),
        P("req", None, "tp"),
        P(),
        P(None, "tp"),
        P(None, "tp"),
        P(None, "tp"),
        P("tp", None),
        P(),
        P(None, "tp"),
        P(None, "tp"),
        P("tp", None),
    )
    return jax.shard_map(
        per_device,
        mesh=mesh,
        in_specs=placed,
        out_specs=(P("req", None), P("req", None, "tp")),
        check_vma=False,
    )
```

profile of v0, /device:TPU:0, one launch (start us, length us, event | category | flops | bytes accessed | tf_op | source)
XLA Modules:
  0.0 1126.5 jit_solution(8354011638535789150)
XLA Ops:
  12.5 18.3 %all-reduce = s32[512]{0:T(512)S(1)} all-reduce(s32[512]{0:T(512)S(1)} %dynamic-update-slice), channel_id=1, replica_groups=mesh['req'=32,'tp'=4] {'req'}, use_global_device_ids=true, to_apply=%add | all-reduce | flops 512 | bytes 4096
  36.3 259.8 %while.44 = (s32[]{:T(128)}, u32[4096]{0:T(1024)S(1)}, u32[4096]{0:T(1024)S(1)}, s32[512]{0:T(512)S(1)}, s32[]{:T(128)}, /*index=5*/s32[]{:T(128)}, s32[]{:T(128)}, s32[]{}) while((s32[]{:T(128)}, u32[4096]{0:T(1024)S(1)}, u32[4096]{0:T(1024)S(1)}, s32[512]{0:T(512)S(1)}, s32[]{:T(128)}, /*index=5*/s32[]{:T(128)}, s32[]{:T(128)}, ...), condition=%wide.region_3.4_spmd.clone, body=%wide.region_2.3_spmd.clone.sunk | while | flops 81924 | bytes 254065 | solution.py:88
  36.3 25.9 %gather_fusion = s32[4096]{0:T(1024)S(1)} fusion(s32[512]{0:T(512)S(1)} %get-tuple-element.479, u32[4096]{0:T(1024)S(1)} %broadcast_clamp_fusion.3), kind=kCustom, calls=%fused_computation.clone.clone.1 | custom fusion | bytes 49152 | tf_op jit(solution)/shard_map/jit(searchsorted)/jit(_searchsorted_scan_impl)/vmap(jit(_searchsorted_scan_impl))/while/body/eval_jaxpr/gather | solution.py:88
  62.3 25.9 %gather_fusion = s32[4096]{0:T(1024)S(1)} fusion(s32[512]{0:T(512)S(1)} %get-tuple-element.479, u32[4096]{0:T(1024)S(1)} %broadcast_clamp_fusion.3), kind=kCustom, calls=%fused_computation.clone.clone.1 | custom fusion | bytes 49152 | tf_op jit(solution)/shard_map/jit(searchsorted)/jit(_searchsorted_scan_impl)/vmap(jit(_searchsorted_scan_impl))/while/body/eval_jaxpr/gather | solution.py:88
  88.2 25.9 %gather_fusion = s32[4096]{0:T(1024)S(1)} fusion(s32[512]{0:T(512)S(1)} %get-tuple-element.479, u32[4096]{0:T(1024)S(1)} %broadcast_clamp_fusion.3), kind=kCustom, calls=%fused_computation.clone.clone.1 | custom fusion | bytes 49152 | tf_op jit(solution)/shard_map/jit(searchsorted)/jit(_searchsorted_scan_impl)/vmap(jit(_searchsorted_scan_impl))/while/body/eval_jaxpr/gather | solution.py:88
  114.2 25.9 %gather_fusion = s32[4096]{0:T(1024)S(1)} fusion(s32[512]{0:T(512)S(1)} %get-tuple-element.479, u32[4096]{0:T(1024)S(1)} %broadcast_clamp_fusion.3), kind=kCustom, calls=%fused_computation.clone.clone.1 | custom fusion | bytes 49152 | tf_op jit(solution)/shard_map/jit(searchsorted)/jit(_searchsorted_scan_impl)/vmap(jit(_searchsorted_scan_impl))/while/body/eval_jaxpr/gather | solution.py:88
  140.2 25.9 %gather_fusion = s32[4096]{0:T(1024)S(1)} fusion(s32[512]{0:T(512)S(1)} %get-tuple-element.479, u32[4096]{0:T(1024)S(1)} %broadcast_clamp_fusion.3), kind=kCustom, calls=%fused_computation.clone.clone.1 | custom fusion | bytes 49152 | tf_op jit(solution)/shard_map/jit(searchsorted)/jit(_searchsorted_scan_impl)/vmap(jit(_searchsorted_scan_impl))/while/body/eval_jaxpr/gather | solution.py:88
  166.2 25.9 %gather_fusion = s32[4096]{0:T(1024)S(1)} fusion(s32[512]{0:T(512)S(1)} %get-tuple-element.479, u32[4096]{0:T(1024)S(1)} %broadcast_clamp_fusion.3), kind=kCustom, calls=%fused_computation.clone.clone.1 | custom fusion | bytes 49152 | tf_op jit(solution)/shard_map/jit(searchsorted)/jit(_searchsorted_scan_impl)/vmap(jit(_searchsorted_scan_impl))/while/body/eval_jaxpr/gather | solution.py:88
  192.2 25.9 %gather_fusion = s32[4096]{0:T(1024)S(1)} fusion(s32[512]{0:T(512)S(1)} %get-tuple-element.479, u32[4096]{0:T(1024)S(1)} %broadcast_clamp_fusion.3), kind=kCustom, calls=%fused_computation.clone.clone.1 | custom fusion | bytes 49152 | tf_op jit(solution)/shard_map/jit(searchsorted)/jit(_searchsorted_scan_impl)/vmap(jit(_searchsorted_scan_impl))/while/body/eval_jaxpr/gather | solution.py:88
  218.1 25.9 %gather_fusion = s32[4096]{0:T(1024)S(1)} fusion(s32[512]{0:T(512)S(1)} %get-tuple-element.479, u32[4096]{0:T(1024)S(1)} %broadcast_clamp_fusion.3), kind=kCustom, calls=%fused_computation.clone.clone.1 | custom fusion | bytes 49152 | tf_op jit(solution)/shard_map/jit(searchsorted)/jit(_searchsorted_scan_impl)/vmap(jit(_searchsorted_scan_impl))/while/body/eval_jaxpr/gather | solution.py:88
  244.1 25.9 %gather_fusion = s32[4096]{0:T(1024)S(1)} fusion(s32[512]{0:T(512)S(1)} %get-tuple-element.479, u32[4096]{0:T(1024)S(1)} %broadcast_clamp_fusion.3), kind=kCustom, calls=%fused_computation.clone.clone.1 | custom fusion | bytes 49152 | tf_op jit(solution)/shard_map/jit(searchsorted)/jit(_searchsorted_scan_impl)/vmap(jit(_searchsorted_scan_impl))/while/body/eval_jaxpr/gather | solution.py:88
  270.1 25.9 %gather_fusion = s32[4096]{0:T(1024)S(1)} fusion(s32[512]{0:T(512)S(1)} %get-tuple-element.479, u32[4096]{0:T(1024)S(1)} %broadcast_clamp_fusion.3), kind=kCustom, calls=%fused_computation.clone.clone.1 | custom fusion | bytes 49152 | tf_op jit(solution)/shard_map/jit(searchsorted)/jit(_searchsorted_scan_impl)/vmap(jit(_searchsorted_scan_impl))/while/body/eval_jaxpr/gather | solution.py:88
  296.7 25.9 %gather_fusion.2 = s32[4096]{0:T(1024)S(1)} fusion(s32[512]{0:T(512)S(1)} %copy-done.1, s32[4096]{0:T(1024)S(1)} %fusion.38), kind=kCustom, calls=%fused_computation.2 | custom fusion | bytes 49152 | tf_op jit(solution)/shard_map/gather | solution.py:89
  328.4 22.2 %all_gather.22 = bf16[512,512]{1,0:T(8,128)(2,1)S(1)} all-gather(bf16[16,512]{1,0:T(8,128)(2,1)S(1)} %bitcast.112), channel_id=1, replica_groups=mesh['req'=32,'tp'=4] {'req'}, dimensions={0}, use_global_device_ids=true | all-gather | bytes 540672 | tf_op jit(solution)/shard_map/all_gather | solution.py:110
  350.6 17.3 %gather_fusion.3 = bf16[4096,512]{1,0:T(8,128)(2,1)} fusion(bf16[512,512]{1,0:T(8,128)(2,1)S(1)} %all_gather.22, s32[4096]{0:T(1024)S(1)} %broadcast_clamp_fusion.1), kind=kCustom, calls=%fused_computation.3 | custom fusion | bytes 8404992 | tf_op jit(solution)/shard_map/gather | solution.py:111
  425.1 14.4 %multiply_select_fusion = f32[4096,2,2]{2,1,0:T(2,128)S(1)} fusion(f32[4096,2,2]{2,1,0:T(2,128)S(1)} %bitcast.97, pred[4096]{0:T(1024)(128)(4,1)S(1)} %broadcast_compare_fusion), kind=kLoop, calls=%fused_computation.39 | loop fusion | flops 32768 | bytes 135168 | tf_op jit(solution)/shard_map/jit(_where)/select_n | solution.py:116
  463.6 28.4 %gather_fusion.4 = f32[4096,2,2]{2,1,0:T(2,128)} fusion(f32[512,2,2]{2,1,0:T(2,128)S(1)} %copy.93, s32[4096]{0:T(1024)S(1)} %broadcast_clamp_fusion.1), kind=kCustom, calls=%fused_computation.4 | custom fusion | bytes 147456 | tf_op jit(solution)/shard_map/gather | solution.py:122
  491.9 16.7 %exponential_select_fusion = f32[4096,2,2]{2,1,0:T(2,128)S(1)} fusion(f32[4096,2,2]{2,1,0:T(2,128)} %gather_fusion.4, pred[4096]{0:T(1024)(128)(4,1)S(1)} %broadcast_compare_fusion, f32[4096,2,2]{2,1,0:T(2,128)} %bitcast.98), kind=kLoop, calls=%fused_computation.38 | loop fusion | flops 65536 | bytes 200704 | tf_op jit(solution)/shard_map/jit(_where)/select_n | solution.py:122
  542.8 25.0 %all-gather = f32[16384,2,2]{0,2,1:T(2,128)S(1)} all-gather(f32[512,2,2]{0,2,1:T(2,128)S(1)} %pad_maximum_fusion.6), channel_id=2, replica_groups=mesh['req'=32,'tp'=4] {'req'}, dimensions={0}, use_global_device_ids=true | all-gather | bytes 270336 | tf_op jit(solution)/shard_map/all_gather | solution.py:17
  576.7 22.4 %all-gather.1 = f32[16384,2,2]{0,2,1:T(2,128)S(1)} all-gather(f32[512,2,2]{0,2,1:T(2,128)S(1)} %fusion.15), channel_id=3, replica_groups=mesh['req'=32,'tp'=4] {'req'}, dimensions={0}, use_global_device_ids=true | all-gather | bytes 270336 | tf_op jit(solution)/shard_map/all_gather | solution.py:17
  603.0 55.4 %all-gather.5.cloned.1.call-done = f32[16384,2,2,128]{3,0,2,1:T(8,128)} async-done(((f32[512,2,2,128]{3,0,2,1:T(8,128)}), f32[16384,2,2,128]{3,0,2,1:T(8,128)}) %all-gather.5.cloned.1.call-update) | async-done | bytes 33554448 | tf_op jit(solution)/shard_map/all_gather | solution.py:17
  661.5 362.1 %while.43 = (s32[]{:T(128)}, f32[512,2,2]{0,2,1:T(2,128)S(1)}, f32[512,2,2]{0,2,1:T(2,128)S(1)}, f32[512,2,2,128]{3,2,1,0:T(2,128)}, f32[32,512,2,2]{1,0,3,2:T(8...) while((s32[]{:T(128)}, f32[512,2,2]{0,2,1:T(2,128)S(1)}, ...), condition=%wide.region_8.9_spmd, body=%wide.region_7.8_spmd.sunk | while | flops 798725 | bytes 5390479 | solution.py:22
  1026.0 40.3 %all-reduce.4.cloned.1.call-done = f32[16,2048]{1,0:T(8,128)} async-done(((f32[16,2048]{1,0:T(8,128)}), f32[16,2048]{1,0:T(8,128)}) %all-reduce.4.cloned.1.call-update) | async-done | bytes 131088 | tf_op jit(solution)/shard_map/psum | solution.py:161
  1077.2 41.0 %all-reduce.6.cloned.1.call-done = f32[16,2048]{1,0:T(8,128)} async-done(((f32[16,2048]{1,0:T(8,128)}), f32[16,2048]{1,0:T(8,128)}) %all-reduce.6.cloned.1.call-update) | async-done | bytes 131088 | tf_op jit(solution)/shard_map/psum | solution.py:167
  (336 shorter events, 524.4 us)
Async XLA Ops:
  7.2 1017.7 %copy-start = (bf16[512,2048]{1,0:T(8,128)(2,1)S(1)}, bf16[512,2048]{1,0:T(8,128)(2,1)}, u32[]{:S(2)}) copy-start(bf16[512,2048]{1,0:T(8,128)(2,1)} %param.29) | copy-start | bytes 6291460
  7.2 651.2 %all-gather.5.cloned.1.call-start = ((), (), s32[]{:S(2)}) async-start(), calls=%async_computation.2 | async-start | bytes 34603008 | tf_op jit(solution)/shard_map/all_gather | solution.py:17
  296.0 0.7 copy-start.1
  322.6 5.1 copy-start.5
  322.6 5.0 copy-start.6
  425.1 14.5 %copy-start.3 = (f32[4096,2,1,2]{3,2,1,0:T(1,128)}, f32[4096,2,1,2]{3,2,1,0:T(1,128)S(1)}, u32[]{:S(2)}) copy-start(f32[4096,2,1,2]{3,2,1,0:T(1,128)S(1)} %fusion.57) | copy-start | bytes 196612
  508.6 5.1 copy-start.2
  518.2 11.7 %copy-start.4 = (bf16[4096,1,256]{0,2,1:T(8,128)(2,1)S(1)}, bf16[4096,1,256]{0,2,1:T(8,128)(2,1)}, u32[]{:S(2)}) copy-start(bf16[4096,1,256]{0,2,1:T(8,128)(2,1)} %copy.117) | copy-start | bytes 6291460
  542.7 523.6 %all-reduce.4.cloned.1.call-start = ((), (), s32[]{:S(2)}) async-start(), calls=%async_computation | async-start | bytes 262144 | tf_op jit(solution)/shard_map/psum | solution.py:161
  567.7 9.0 copy-start.8
  599.1 62.3 %slice-start = ((f32[16384,2,2]{0,2,1:T(2,128)}), f32[512,2,2]{0,2,1:T(2,128)S(1)}, s32[]{:S(2)}) async-start(f32[16384,2,2]{0,2,1:T(2,128)} %copy-done.8), calls=%async_computation.3 | async-start | bytes 16384 | tf_op jit(solution)/shard_map/jit(dynamic_index_in_dim)/dynamic_slice | solution.py:20
  661.5 364.5 %copy-start.9 = (bf16[2048]{0:T(1024)(128)(2,1)S(1)}, bf16[2048]{0:T(1024)(128)(2,1)}, u32[]{:S(2)}) copy-start(bf16[2048]{0:T(1024)(128)(2,1)} %param.30) | copy-start | bytes 12292
  1025.9 92.3 %all-reduce.6.cloned.1.call-start = ((), (), s32[]{:S(2)}) async-start(), calls=%async_computation.1 | async-start | bytes 262144 | tf_op jit(solution)/shard_map/psum | solution.py:167
  1071.2 47.1 %copy-start.7 = (f32[16,2048]{1,0:T(8,128)S(1)}, f32[16,2048]{1,0:T(8,128)}, u32[]{:S(2)}) copy-start(f32[16,2048]{1,0:T(8,128)} %all-reduce.4.cloned.1.call-done) | copy-start | bytes 393220
Sparse Core Ops, SparseCore 0:
  542.8 115.5 all-gather.4
  1026.0 40.1 all-reduce.3
  1076.7 41.5 all-reduce.5
where the time goes:
time: 1130 us
  local copies, waits for them, and re-layouts  505 us (45%)
  other arithmetic  331 us (29%)
  waiting for transfers between devices  137 us (12%)
  blocking collectives  87.8 us (8%)
  matrix products  50 us (4%)
  between operations  15 us (1%)
    add x31, other arithmetic, combine_parts(): first[2] * left[..., None] + second[2] * right[..., None]  277 us
    gather x10, local copies, waits for them, and re-layouts, per_device(): place = jnp.searchsorted(ends, slot_ids, side='right')  259 us
    dynamic_slice x66, local copies, waits for them, and re-layouts, take(): lax.dynamic_index_in_dim(a, source, 0, False)  68.2 us
    all_gather x1, waiting for transfers between devices, joined(): gathered = jax.tree.map(lambda a: lax.all_gather(a, axis), part)  55.4 us
    all_gather x2, blocking collectives, joined(): gathered = jax.tree.map(lambda a: lax.all_gather(a, axis), part)  47.4 us
    psum x1, waiting for transfers between devices, per_device(): hidden_out = mid + lax.psum(down_part, 'tp')  41 us
    psum x1, waiting for transfers between devices, per_device(): mid = rows + lax.psum(partial_attn, 'tp')  40.3 us
    gather x1, local copies, waits for them, and re-layouts, per_device(): weights = jnp.where(live, jnp.exp(scores - peak[owner]), 0.0)  28.4 us
  transfers between devices with their start and end apart: 3, of which 3 were waited for; matrix products, arithmetic and copies ran while one was open for 1% of the time, Pallas kernels for 0%

commit v1 on v0

v1 whole, which is shorter than its diff:
```python
import functools
import math

import jax
import jax.numpy as jnp
import numpy as np
from jax import lax
from jax.experimental import pallas as pl
from jax.experimental.pallas import tpu as pltpu
from jax.sharding import PartitionSpec as P

MESH = pl.DeviceIdType.MESH
HEAD_DIM = 128
ROPE_BASE = 1000000.0
EPS = 1e-05
FLOOR = -1e30
SCALE = 1.0 / math.sqrt(HEAD_DIM)
SIDE = 4
CHIPS = SIDE * SIDE
ROWS = 16
REQS = 512
SLOTS = 4096
HALF = REQS // 2
QW = 512
PW = QW + 128
WIN = 32
BF16 = jnp.bfloat16
F32 = jnp.float32


def place():
    me = lax.axis_index("req")
    core = lax.rem(me, 2)
    chip = me // 2
    return core, chip // SIDE, lax.rem(chip, SIDE), lax.axis_index("tp")


def chip_at(y, z, k):
    return lax.rem(y + k // SIDE, SIDE) * SIDE + lax.rem(z + k % SIDE, SIDE)


def device(chip, core, tp):
    return {"req": chip * 2 + core, "tp": tp}


def rms_norm(rows, gain):
    mean_sq = jnp.mean(rows * rows, axis=-1, keepdims=True)
    return rows * lax.rsqrt(mean_sq + EPS) * gain.astype(F32)


def frequency_table():
    half = HEAD_DIM // 2
    turns = ROPE_BASE ** (-(np.arange(half, dtype=np.float64) * 2.0) / HEAD_DIM) / (2.0 * np.pi)
    first = np.round(turns * 2.0**12) / 2.0**12
    second = np.round((turns - first) * 2.0**23) / 2.0**23
    third = turns - first - second
    table = np.zeros((8, HEAD_DIM), np.float64)
    for i, term in enumerate((first, second, third)):
        table[i] = np.concatenate([term, term])
    return table.astype(np.float32)


def cos_sin(where, table):
    turn = where * table[0:1, :]
    turn = turn - jnp.floor(turn + 0.5)
    turn = turn + where * table[1:2, :]
    turn = turn - jnp.floor(turn + 0.5)
    turn = turn + where * table[2:3, :]
    quarter = jnp.floor(turn * 4.0 + 0.5)
    x = (turn - quarter * 0.25) * np.float32(2.0 * np.pi)
    sq = x * x
    sine = x * (1.0 + sq * (-1.0 / 6 + sq * (1.0 / 120 + sq * (-1.0 / 5040 + sq * (1.0 / 362880)))))
    cosine = 1.0 + sq * (
        -0.5 + sq * (1.0 / 24 + sq * (-1.0 / 720 + sq * (1.0 / 40320 + sq * (-1.0 / 3628800))))
    )
    odd = (quarter == 1.0) | (quarter == -1.0)
    far = (quarter == 2.0) | (quarter == -2.0)
    c = jnp.where(odd, -quarter * sine, jnp.where(far, -cosine, cosine))
    s = jnp.where(odd, quarter * cosine, jnp.where(far, -sine, sine))
    return c, s


def project_kernel(
    len_s, pos_s, tok, gain, table, wq_h, wk_h, wv_h, pool_h,
    qall_o, lens_o, qown_o, newkv_o, kvd_o,
    wq, wk, wv, pool, kvd, tmp, qall, lens,
    w_sem, pool_sem, out_sem, ls_sem, lr_sem, lf_sem, qs_sem, qr_sem, fs_sem, fr_sem,
):
    core, y, z, tp = place()
    chip = y * SIDE + z
    loads = [
        pltpu.make_async_copy(src, dst, w_sem.at[i])
        for i, (src, dst) in enumerate(((wq_h, wq), (wk_h, wk), (wv_h, wv)))
    ]
    piece = 4 * SLOTS // 4
    pool_loads = [
        pltpu.make_async_copy(pool_h.at[pl.ds(i * piece, piece)], pool.at[pl.ds(i * piece, piece)], pool_sem.at[i])
        for i in range(4)
    ]
    for copy in loads + pool_loads:
        copy.start()

    barrier = pltpu.get_barrier_semaphore()
    sibling = device(chip, 1 - core, tp)
    peers = [sibling] + [device(chip_at(y, z, k), core, tp) for k in range(1, CHIPS)]
    for peer in peers:
        pl.semaphore_signal(barrier, inc=1, device_id=peer, device_id_type=MESH)

    lane = lax.broadcasted_iota(jnp.int32, (1, 128), 1)
    mine = jnp.zeros((1, 128), jnp.int32)
    first_lane = lax.rem(chip, 8) * ROWS
    for i in range(ROWS):
        mine = jnp.where(lane == first_lane + i, len_s[i], mine)
    lens[pl.ds(core * CHIPS + chip, 1), :] = mine

    row = lax.broadcasted_iota(jnp.int32, (ROWS, 128), 0)
    where = jnp.zeros((ROWS, 128), jnp.int32)
    for i in range(ROWS):
        where = jnp.where(row == i, pos_s[i], where)
    cosine, sine = cos_sin(where.astype(F32), table[...])
    low = lax.broadcasted_iota(jnp.int32, (ROWS, 128), 1) < HEAD_DIM // 2
    sine = jnp.where(low, -sine, sine)

    def rotate(vectors):
        return vectors * cosine + pltpu.roll(vectors, HEAD_DIM // 2, axis=1) * sine

    normed = rms_norm(tok[...].astype(F32), gain[...]).astype(BF16)

    pl.semaphore_wait(barrier, len(peers))
    my_len = lens.at[pl.ds(core * CHIPS + chip, 1)]
    len_sends = [
        pltpu.make_async_remote_copy(
            src_ref=my_len, dst_ref=my_len, send_sem=ls_sem.at[k], recv_sem=lr_sem.at[k],
            device_id=peers[k], device_id_type=MESH,
        )
        for k in range(1, CHIPS)
    ]
    for copy in len_sends:
        copy.start()

    loads[0].wait()
    query = jnp.dot(normed, wq[...], preferred_element_type=F32)
    mine_at = pl.multiple_of(core * HALF + chip * ROWS, ROWS)
    for h in range(QW // HEAD_DIM):
        cols = pl.ds(h * HEAD_DIM, HEAD_DIM)
        turned = rotate(query[:, h * HEAD_DIM:(h + 1) * HEAD_DIM]).astype(BF16)
        qall[pl.ds(mine_at, ROWS), cols] = turned
        qown_o[:, cols] = turned
    my_rows = qall.at[pl.ds(mine_at, ROWS)]
    q_sends = []
    for k in (10, 5, 7, 13, 15, 2, 8, 6, 14, 9, 11, 1, 3, 4, 12):
        q_sends.append(
            pltpu.make_async_remote_copy(
                src_ref=my_rows, dst_ref=my_rows, send_sem=qs_sem.at[k], recv_sem=qr_sem.at[k],
                device_id=peers[k], device_id_type=MESH,
            )
        )

    def forward(k):
        source = lax.rem(y + SIDE - k // SIDE, SIDE) * SIDE + lax.rem(z + SIDE - k % SIDE, SIDE)
        rows = qall.at[pl.ds(pl.multiple_of(core * HALF + source * ROWS, ROWS), ROWS)]
        return pltpu.make_async_remote_copy(
            src_ref=rows, dst_ref=rows, send_sem=fs_sem.at[k], recv_sem=fr_sem.at[k],
            device_id=sibling, device_id_type=MESH,
        )

    for copy in q_sends:
        copy.start()
    forwards = [forward(0)]
    forwards[0].start()

    loads[1].wait()
    key = jnp.dot(normed, wk[...], preferred_element_type=F32)
    loads[2].wait()
    value = jnp.dot(normed, wv[...], preferred_element_type=F32)
    for h in range(2):
        cols = slice(h * HEAD_DIM, (h + 1) * HEAD_DIM)
        newkv_o[pl.ds(2 * h, ROWS, stride=4), :] = rotate(key[:, cols])
        newkv_o[pl.ds(2 * h + 1, ROWS, stride=4), :] = value[:, cols]

    for copy in len_sends:
        copy.wait()
    group = lens.at[pl.ds(pl.multiple_of(core * CHIPS, CHIPS), CHIPS)]
    len_forward = pltpu.make_async_remote_copy(
        src_ref=group, dst_ref=group, send_sem=lf_sem.at[0], recv_sem=lf_sem.at[1],
        device_id=sibling, device_id_type=MESH,
    )
    len_forward.start()

    def untangle(i):
        tmp[...] = pool[pl.ds(i * 1024, 1024), :].astype(F32)
        for j in range(4):
            kvd[pl.ds(i * 256, 256), pl.ds(j * 128, 128)] = tmp[pl.ds(j, 256, stride=4), :].astype(BF16)

    for i in range(4):
        pool_loads[i].wait()
    outs = []
    order = (1, 3, 4, 12, 2, 8, 5, 7, 13, 15, 6, 14, 9, 11, 10)
    sends = dict(zip((10, 5, 7, 13, 15, 2, 8, 6, 14, 9, 11, 1, 3, 4, 12), q_sends))
    for i in range(16):
        if i < len(order):
            k = order[i]
            sends[k].wait_recv()
            forwards.append(forward(k))
            forwards[-1].start()
        untangle(i)
        if i % 4 == 3:
            rows = pl.ds((i - 3) * 256, 1024)
            outs.append(pltpu.make_async_copy(kvd.at[rows], kvd_o.at[rows], out_sem.at[i // 4]))
            outs[-1].start()
    len_forward.wait()
    lens_o[...] = lens[...]
    for copy in forwards:
        copy.wait()
    last = pltpu.make_async_copy(qall, qall_o, out_sem.at[4])
    last.start()
    for copy in q_sends:
        copy.wait_send()
    for copy in outs:
        copy.wait()
    last.wait()


def attend_kernel(
    base_s, qall, lens, order, mask, kvd_h, part,
    kvd, scores, order_b, first_b, last_b, pooled, kv_sem,
):
    loads = []
    for i in range(8):
        rows = pl.ds(i * 512, 512)
        loads.append(pltpu.make_async_copy(kvd_h.at[rows], kvd.at[rows], kv_sem.at[i]))
        loads[-1].start()
    base = base_s[0]

    def request_of(n):
        return ((n >> 4) & 15) * 32 + (n >> 8) * 16 + (n & 15)

    n_lane = [request_of(lax.broadcasted_iota(jnp.int32, (1, 128), 1) + 128 * t) for t in range(4)]
    len_lane = [jnp.sum(lens[8 * t:8 * t + 8, :], axis=0, keepdims=True).astype(F32) for t in range(4)]
    pos_lane = [jnp.zeros((1, 128), F32) for _ in range(4)]
    for t in range(4):
        tile = jnp.broadcast_to(order[t:t + 1, :], (128, 128)).astype(F32)
        order_b[pl.ds(128 * t, 128), :] = jnp.transpose(tile).astype(jnp.int32)
    p_sub = lax.broadcasted_iota(jnp.int32, (REQS, 128), 0).astype(F32)
    for t in range(4):
        here = order_b[...] == n_lane[t]
        pos_lane[t] = jnp.sum(jnp.where(here, p_sub, 0.0), axis=0, keepdims=True)
    upto = jnp.zeros((REQS, 128), F32)
    before = jnp.zeros((REQS, 128), F32)
    for t in range(4):
        upto += jnp.where(pos_lane[t] <= p_sub, len_lane[t], 0.0)
        before += jnp.where(pos_lane[t] < p_sub, len_lane[t], 0.0)
    ends = jnp.sum(upto, axis=1, keepdims=True).astype(jnp.int32) - base
    starts = jnp.sum(before, axis=1, keepdims=True).astype(jnp.int32) - base
    first_b[...] = jnp.broadcast_to(starts, (REQS, 128))
    last_b[...] = jnp.broadcast_to(ends, (REQS, 128))
    low = jnp.sum((ends <= 0).astype(jnp.int32))
    high = jnp.sum((starts < SLOTS).astype(jnp.int32))
    low = (low // 16) * 16
    windows = (high - low + (WIN - 1)) // WIN

    pooled[...] = jnp.zeros_like(pooled)
    for copy in loads:
        copy.wait()

    slot = lax.broadcasted_iota(jnp.int32, (8, 128), 1)

    @pl.loop(0, windows)
    def _(w):
        at = pl.multiple_of(jnp.minimum(low + w * WIN, REQS - WIN), 16)
        own = order_b[pl.ds(at, WIN), :]
        pick = jnp.concatenate([(own == n_lane[t]).astype(F32).astype(BF16) for t in range(4)], axis=1)
        query = jnp.dot(pick, qall[...], preferred_element_type=F32).astype(BF16)
        first = first_b[pl.ds(at, WIN), :]
        last = last_b[pl.ds(at, WIN), :]
        first = jnp.concatenate([first, first], axis=0)
        last = jnp.concatenate([last, last], axis=0)
        stats = jnp.zeros((WIN, 128), F32)
        lane = lax.broadcasted_iota(jnp.int32, (WIN, 128), 1)
        for j in range(2):
            q = jnp.concatenate(
                [query[:, (2 * j + g) * HEAD_DIM:(2 * j + g + 1) * HEAD_DIM] for g in range(2)], axis=0
            )

            def score(c, peak):
                start = pl.multiple_of(c * 512, 512)
                keys = kvd[pl.ds(start, 512), pl.ds(2 * j * 128, 128)]
                s = lax.dot_general(q, keys, (((1,), (1,)), ((), ())), preferred_element_type=F32) * SCALE
                for i in range(4):
                    live = mask[pl.ds(c * 4 + i, 1), :] == 1
                    index = jnp.where(live, slot[0:1, :] + (c * 512 + i * 128), -REQS * 8192)
                    ok = (index >= first) & (index < last)
                    part_s = jnp.where(ok, s[:, i * 128:(i + 1) * 128], FLOOR)
                    scores[:, pl.ds(pl.multiple_of(start + i * 128, 128), 128)] = part_s
                    peak = jnp.maximum(peak, part_s)
                return peak

            peak = lax.fori_loop(0, 8, score, jnp.full((2 * WIN, 128), FLOOR, F32))
            peak = jnp.max(peak, axis=1, keepdims=True)
            peak = jnp.where(peak > 0.5 * FLOOR, peak, 0.0)

            def weigh(c, state):
                total, summed = state
                start = pl.multiple_of(c * 512, 512)
                weight = jnp.exp(scores[:, pl.ds(start, 512)] - peak).astype(BF16)
                values = kvd[pl.ds(start, 512), pl.ds((2 * j + 1) * 128, 128)]
                summed = summed + jnp.dot(weight, values, preferred_element_type=F32)
                wide = weight.astype(F32)
                for i in range(4):
                    total = total + wide[:, i * 128:(i + 1) * 128]
                return total, summed

            zero = jnp.zeros((2 * WIN, 128), F32)
            total, summed = lax.fori_loop(0, 8, weigh, (zero, zero))
            total = jnp.sum(total, axis=1, keepdims=True)
            mean = (summed / jnp.where(total > 0.0, total, 1.0)).astype(BF16)
            for g in range(2):
                h = 2 * j + g
                pooled[pl.ds(at, WIN), pl.ds(h * HEAD_DIM, HEAD_DIM)] = mean[g * WIN:(g + 1) * WIN]
                stats = jnp.where(lane == h, peak[g * WIN:(g + 1) * WIN], stats)
                stats = jnp.where(lane == 4 + h, total[g * WIN:(g + 1) * WIN], stats)
        pooled[pl.ds(at, WIN), pl.ds(QW, 128)] = pack_stats(stats)

    n_sub = request_of(lax.broadcasted_iota(jnp.int32, (REQS, 128), 0))
    place_n = jnp.concatenate([(order[t:t + 1, :] == n_sub).astype(F32).astype(BF16) for t in range(4)], axis=1)
    part[...] = jnp.dot(place_n, pooled[...], preferred_element_type=F32).astype(BF16)


def pack_stats(stats):
    top = stats.astype(BF16).astype(F32)
    rest = stats - top
    middle = rest.astype(BF16).astype(F32)
    rest = rest - middle
    return (top + pltpu.roll(middle, 8, axis=1) + pltpu.roll(rest, 16, axis=1)).astype(BF16)


def peaks_totals(tile):
    tile = tile.astype(F32)
    values = tile + pltpu.roll(tile, 120, axis=1) + pltpu.roll(tile, 112, axis=1)
    totals = pltpu.roll(values, 124, axis=1)
    return jnp.where(totals > 0.0, values, FLOOR), totals


def head(block, h):
    return block[:, h * HEAD_DIM:(h + 1) * HEAD_DIM]


def finish_kernel(
    part_h, qown, newkv, tok, gain, wo_h, wg_h, wu_h, wd_h, out,
    own, came, comb, rx, mix, down, wo, wg, wu, wd,
    w_sem, own_sem, ps_sem, pr_sem, cs_sem, cr_sem, ms_sem, mr_sem, ds_sem, dr_sem,
):
    core, y, z, tp = place()
    chip = y * SIDE + z
    barrier = pltpu.get_barrier_semaphore()
    sibling = device(chip, 1 - core, tp)
    peers = [sibling] + [device(chip_at(y, z, k), core, tp) for k in range(1, CHIPS)]
    beside = [device(chip, core, lax.rem(tp + d, 4)) for d in range(1, 4)]
    for peer in peers + beside:
        pl.semaphore_signal(barrier, inc=1, device_id=peer, device_id_type=MESH)
    mine = pltpu.make_async_copy(part_h.at[pl.ds(pl.multiple_of(core * HALF, HALF), HALF)], own, own_sem)
    mine.start()
    pl.semaphore_wait(barrier, len(peers) + len(beside))

    def rows_of(dy):
        return pl.multiple_of(lax.rem(y + dy, SIDE) * 64, 64)

    turns = (2, 1, 3, 0)
    swaps = []
    for dy in turns:
        swaps.append(
            pltpu.make_async_remote_copy(
                src_ref=part_h.at[pl.ds(pl.multiple_of((1 - core) * HALF + rows_of(dy), 64), 64)],
                dst_ref=came.at[pl.ds(rows_of(dy), 64)],
                send_sem=ps_sem.at[dy], recv_sem=pr_sem.at[dy], device_id=sibling, device_id_type=MESH,
            )
        )
        swaps[-1].start()
    loads = [
        pltpu.make_async_copy(src, dst, w_sem.at[i])
        for i, (src, dst) in enumerate(((wo_h, wo), (wg_h, wg), (wu_h, wu), (wd_h, wd)))
    ]
    for copy in loads:
        copy.start()

    mine.wait()
    lane64 = lax.broadcasted_iota(jnp.int32, (64, 128), 1)
    sends = []
    for dy, swap in zip(turns, swaps):
        swap.wait_recv()
        rows = pl.ds(rows_of(dy), 64)
        peak_a, total_a = peaks_totals(own[rows, pl.ds(QW, 128)])
        peak_b, total_b = peaks_totals(came[rows, pl.ds(QW, 128)])
        peak = jnp.maximum(peak_a, peak_b)
        left = total_a * jnp.exp(peak_a - peak)
        right = total_b * jnp.exp(peak_b - peak)
        total = left + right
        share = 1.0 / jnp.where(total > 0.0, total, 1.0)
        for h in range(4):
            cols = pl.ds(h * HEAD_DIM, HEAD_DIM)
            comb[rows, cols] = (
                own[rows, cols].astype(F32) * (left * share)[:, h:h + 1]
                + came[rows, cols].astype(F32) * (right * share)[:, h:h + 1]
            ).astype(BF16)
        stats = jnp.where(lane64 < 4, jnp.where(total > 0.0, peak, 0.0), 0.0)
        shifted = pltpu.roll(jnp.where(lane64 < 4, total, 0.0), 4, axis=1)
        comb[rows, pl.ds(QW, 128)] = pack_stats(stats + shifted)
        for dz in (2, 1, 3, 0):
            k = dy * SIDE + dz
            if k == 0:
                continue
            block = comb.at[pl.ds(pl.multiple_of(chip_at(y, z, k) * ROWS, ROWS), ROWS)]
            sends.append(
                pltpu.make_async_remote_copy(
                    src_ref=block, dst_ref=rx.at[k], send_sem=cs_sem.at[k], recv_sem=cr_sem.at[k],
                    device_id=peers[k], device_id_type=MESH,
                )
            )
            sends[-1].start()

    peaks, totals, blocks = [], [], []
    for h in range(4):
        keys = newkv[pl.ds(2 * (h // 2), ROWS, stride=4), :].astype(BF16).astype(F32)
        query = head(qown[...], h).astype(F32)
        peaks.append(jnp.sum(query * keys, axis=1, keepdims=True) * SCALE)
    lane = lax.broadcasted_iota(jnp.int32, (ROWS, 128), 1)
    own_peak = jnp.full((ROWS, 128), FLOOR, F32)
    for h in range(4):
        own_peak = jnp.where(lane == h, peaks[h], own_peak)

    for copy in sends:
        copy.wait_recv()
    mine_rows = pl.ds(pl.multiple_of(chip * ROWS, ROWS), ROWS)

    def block_of(k, cols):
        return comb[mine_rows, cols] if k == 0 else rx[k, :, cols]

    found = [peaks_totals(block_of(k, pl.ds(QW, 128))) for k in range(CHIPS)]
    peak = own_peak
    for other, _ in found:
        peak = jnp.maximum(peak, other)
    scales = [total * jnp.exp(other - peak) for other, total in found]
    own_scale = jnp.where(lane < 4, jnp.exp(own_peak - peak), 0.0)
    total = own_scale
    for one in scales:
        total = total + one
    total = jnp.where(lane < 4, total, 1.0)
    context = []
    for h in range(4):
        cols = pl.ds(h * HEAD_DIM, HEAD_DIM)
        values = newkv[pl.ds(2 * (h // 2) + 1, ROWS, stride=4), :].astype(BF16).astype(F32)
        summed = own_scale[:, h:h + 1] * values
        for k in range(CHIPS):
            summed = summed + scales[k][:, h:h + 1] * block_of(k, cols).astype(F32)
        context.append((summed / total[:, h:h + 1]).astype(BF16))
    context = jnp.concatenate(context, axis=1)

    def over_tp(left, right, width, terms, send, recv):
        copies = []
        for n in range(4):
            cols = pl.ds(n * width, width)
            terms[tp, :, cols] = jnp.dot(left, right[:, cols], preferred_element_type=F32).astype(BF16)
            for d in range(3):
                ref = terms.at[tp, :, cols]
                copies.append(
                    pltpu.make_async_remote_copy(
                        src_ref=ref, dst_ref=ref, send_sem=send.at[n, d], recv_sem=recv.at[n, d],
                        device_id=beside[d], device_id_type=MESH,
                    )
                )
                copies[-1].start()
        return copies

    def summed_terms(terms):
        total = terms[0].astype(F32)
        for t in range(1, 4):
            total = total + terms[t].astype(F32)
        return total

    loads[0].wait()
    mixes = over_tp(context, wo, 512, mix, ms_sem, mr_sem)
    for copy in mixes:
        copy.wait_recv()
    mid = tok[...].astype(F32) + summed_terms(mix)
    normed = rms_norm(mid, gain[...]).astype(BF16)
    loads[1].wait()
    loads[2].wait()
    acts = []
    for n in range(2):
        cols = pl.ds(n * 512, 512)
        gate = jnp.dot(normed, wg[:, cols], preferred_element_type=F32)
        upper = jnp.dot(normed, wu[:, cols], preferred_element_type=F32)
        acts.append((gate / (1.0 + jnp.exp(-gate)) * upper).astype(BF16))
    act = jnp.concatenate(acts, axis=1)
    loads[3].wait()
    downs = over_tp(act, wd, 512, down, ds_sem, dr_sem)
    for copy in downs:
        copy.wait_recv()
    out[...] = mid + summed_terms(down)
    for copy in swaps + sends + mixes + downs:
        copy.wait_send()


def per_device(
    tokens, lengths, pool_order, positions, slot_mask, kv_cache, attn_gain,
    w_query, w_key, w_value, w_out, ffn_gain, w_gate, w_up, w_down,
):
    vmem = pl.BlockSpec(memory_space=pltpu.VMEM)
    smem = pl.BlockSpec(memory_space=pltpu.SMEM)
    hbm = pl.BlockSpec(memory_space=pl.ANY)
    dma = pltpu.SemaphoreType.DMA
    pool = kv_cache.reshape(SLOTS, 2, 2, HEAD_DIM).transpose(0, 2, 1, 3).reshape(4 * SLOTS, HEAD_DIM)
    qall, lens, qown, newkv, kvd = pl.pallas_call(
        project_kernel,
        out_shape=(
            jax.ShapeDtypeStruct((REQS, QW), BF16),
            jax.ShapeDtypeStruct((32, 128), jnp.int32),
            jax.ShapeDtypeStruct((ROWS, QW), BF16),
            jax.ShapeDtypeStruct((4 * ROWS, HEAD_DIM), F32),
            jax.ShapeDtypeStruct((SLOTS, QW), BF16),
        ),
        in_specs=[smem, smem, vmem, vmem, vmem, hbm, hbm, hbm, hbm],
        out_specs=(hbm, vmem, vmem, vmem, hbm),
        scratch_shapes=[
            pltpu.VMEM((2048, 512), BF16),
            pltpu.VMEM((2048, 256), BF16),
            pltpu.VMEM((2048, 256), BF16),
            pltpu.VMEM((4 * SLOTS, HEAD_DIM), BF16),
            pltpu.VMEM((SLOTS, QW), BF16),
            pltpu.VMEM((1024, HEAD_DIM), F32),
            pltpu.VMEM((REQS, QW), BF16),
            pltpu.VMEM((32, 128), jnp.int32),
            dma((3,)), dma((4,)), dma((5,)), dma((16,)), dma((16,)), dma((2,)),
            dma((16,)), dma((16,)), dma((16,)), dma((16,)),
        ],
        compiler_params=pltpu.CompilerParams(
            collective_id=0, has_side_effects=True, vmem_limit_bytes=40 << 20
        ),
        name="project",
    )(
        lengths, positions, tokens, attn_gain.reshape(1, -1), jnp.asarray(frequency_table()),
        w_query, w_key, w_value, pool,
    )
    base = (lax.axis_index("req") * SLOTS).astype(jnp.int32).reshape(1)
    part = pl.pallas_call(
        attend_kernel,
        out_shape=jax.ShapeDtypeStruct((REQS, PW), BF16),
        in_specs=[smem, vmem, vmem, vmem, vmem, hbm],
        out_specs=vmem,
        scratch_shapes=[
            pltpu.VMEM((SLOTS, QW), BF16),
            pltpu.VMEM((2 * WIN, SLOTS), F32),
            pltpu.VMEM((REQS, 128), jnp.int32),
            pltpu.VMEM((REQS, 128), jnp.int32),
            pltpu.VMEM((REQS, 128), jnp.int32),
            pltpu.VMEM((REQS, PW), BF16),
            dma((8,)),
        ],
        compiler_params=pltpu.CompilerParams(vmem_limit_bytes=40 << 20),
        name="attend",
    )(base, qall, lens, pool_order.reshape(4, 128), slot_mask.reshape(32, 128), kvd)
    hidden = pl.pallas_call(
        finish_kernel,
        out_shape=jax.ShapeDtypeStruct((ROWS, 2048), F32),
        in_specs=[hbm, vmem, vmem, vmem, vmem, hbm, hbm, hbm, hbm],
        out_specs=vmem,
        scratch_shapes=[
            pltpu.VMEM((HALF, PW), BF16),
            pltpu.VMEM((HALF, PW), BF16),
            pltpu.VMEM((HALF, PW), BF16),
            pltpu.VMEM((CHIPS, ROWS, PW), BF16),
            pltpu.VMEM((4, ROWS, 2048), BF16),
            pltpu.VMEM((4, ROWS, 2048), BF16),
            pltpu.VMEM((512, 2048), BF16),
            pltpu.VMEM((2048, 1024), BF16),
            pltpu.VMEM((2048, 1024), BF16),
            pltpu.VMEM((1024, 2048), BF16),
            dma((4,)), dma, dma((4,)), dma((4,)), dma((16,)), dma((16,)),
            dma((4, 3)), dma((4, 3)), dma((4, 3)), dma((4, 3)),
        ],
        compiler_params=pltpu.CompilerParams(
            collective_id=1, has_side_effects=True, vmem_limit_bytes=40 << 20
        ),
        name="finish",
    )(part, qown, newkv, tokens, ffn_gain.reshape(1, -1), w_out, w_gate, w_up, w_down)
    new_kv = newkv.reshape(ROWS, 2, 2, HEAD_DIM).transpose(0, 2, 1, 3).reshape(ROWS, 2, 256)
    return hidden, new_kv


def solution(mesh):
    placed = (
        P("req", None), P("req"), P(), P("req"), P("req"), P("req", None, "tp"), P(),
        P(None, "tp"), P(None, "tp"), P(None, "tp"), P("tp", None), P(),
        P(None, "tp"), P(None, "tp"), P("tp", None),
    )
    return jax.shard_map(
        per_device,
        mesh=mesh,
        in_specs=placed,
        out_specs=(P("req", None), P("req", None, "tp")),
        check_vma=False,
    )
```

time: 1130 us -> 73.8 us (0.07)
  local copies, waits for them, and re-layouts: 505 us -> 17.4 us
  other arithmetic: 331 us -> 0 us
  waiting for transfers between devices: 137 us -> 0 us
  blocking collectives: 87.8 us -> 0 us
  Pallas kernels: 0 us -> 55.2 us
  matrix products: 50 us -> 0 us
  between operations: 15 us -> 0.73 us
    gather x14 -> x0, local copies, waits for them, and re-layouts: 334 us -> none  [the longest x10 259 us: per_device(): place = jnp.searchsorted(ends, slot_ids, side='right')]
    add x64 -> x0, other arithmetic: 280 us -> none  [the longest x31 277 us: combine_parts(): first[2] * left[..., None] + second[2] * right[..., None]]
    psum x2 -> x0, waiting for transfers between devices: 81.3 us -> none  [the longest x1 41 us: per_device(): hidden_out = mid + lax.psum(down_part, 'tp')]
    all_gather x3 -> x0, blocking collectives: 69.6 us -> none  [the longest x2 47.4 us: joined(): gathered = jax.tree.map(lambda a: lax.all_gather(a, axis), part)]
    dynamic_slice x66 -> x0, local copies, waits for them, and re-layouts: 68.2 us -> none  [take(): lax.dynamic_index_in_dim(a, source, 0, False)]
    all_gather x1 -> x0, waiting for transfers between devices: 55.4 us -> none  [joined(): gathered = jax.tree.map(lambda a: lax.all_gather(a, axis), part)]
    pallas_call x0 -> x3, Pallas kernels: none -> 55.2 us  [the longest x1 31.8 us: per_device(): pl.pallas_call(finish_kernel, out_shape=jax.ShapeDtypeStruct((ROWS, 2048)...]
    dot_general x11 -> x0, matrix products: 50 us -> none  [the longest x2 23.4 us: per_device(): jnp.einsum('srg,sd->rgd', spread, head_values, precision=highest, preferr...]
  transfers between devices with their start and end apart: 3 -> 0, of which waited for: 3 -> 0; matrix products, arithmetic and copies ran while one was open for 1% -> 0% of each run, Pallas kernels for 0% -> 0%
where the time goes in v1:
time: 73.8 us; the launch traced here: 73.4 us
  Pallas kernels  55.2 us (75%)
  local copies, waits for them, and re-layouts  17.4 us (24%)
    pallas_call x1, Pallas kernels, per_device(): pl.pallas_call(finish_kernel, out_shape=jax.ShapeDtypeStruct((ROWS, 2048)...  31.8 us
    unnamed x36, local copies, waits for them, and re-layouts  16.7 us
    pallas_call x1, Pallas kernels, per_device(): pl.pallas_call(project_kernel, out_shape=(jax.ShapeDtypeStruct((REQS, QW)...  15.7 us
    pallas_call x1, Pallas kernels, per_device(): pl.pallas_call(attend_kernel, out_shape=jax.ShapeDtypeStruct((REQS, PW),...  7.7 us

profile of v1, /device:TPU:0, one launch (start us, length us, event | category | flops | bytes accessed | tf_op | source)
XLA Modules:
  0.0 73.4 jit_solution(5774168249269744892)
XLA Ops:
  0.6 0.7 reshape.32.gain
  1.3 2.2 %copy-done = bf16[4096,2,256]{2,1,0:T(2,128)(2,1)S(1)} copy-done((bf16[4096,2,256]{2,1,0:T(2,128)(2,1)S(1)}, bf16[4096,2,256]{2,1,0:T(2,128)(2,1)}, u32[]{:S(2)}) %copy-start) | copy-done | bytes 4194328
  3.5 1.6 %copy-done.5 = bf16[2048,512]{1,0:T(8,128)(2,1)S(1)} copy-done((bf16[2048,512]{1,0:T(8,128)(2,1)S(1)}, bf16[2048,512]{1,0:T(8,128)(2,1)}, u32[]{:S(2)}) %copy-start.5) | copy-done | bytes 2097176
  5.1 1.2 %copy-done.7 = bf16[2048,256]{1,0:T(8,128)(2,1)S(1)} copy-done((bf16[2048,256]{1,0:T(8,128)(2,1)S(1)}, bf16[2048,256]{1,0:T(8,128)(2,1)}, u32[]{:S(2)}) %copy-start.7) | copy-done | bytes 1048600
  6.3 1.2 %copy-done.8 = bf16[2048,256]{1,0:T(8,128)(2,1)S(1)} copy-done((bf16[2048,256]{1,0:T(8,128)(2,1)S(1)}, bf16[2048,256]{1,0:T(8,128)(2,1)}, u32[]{:S(2)}) %copy-start.8) | copy-done | bytes 1048600
  7.6 0.8 %copy-done.9 = bf16[16,2048]{1,0:T(8,128)(2,1)S(1)} copy-done((bf16[16,2048]{1,0:T(8,128)(2,1)S(1)}, bf16[16,2048]{1,0:T(8,128)(2,1)}, u32[]{:S(2)}) %copy-start.9) | copy-done | bytes 65560
  8.4 0.7 copy-done.12
  9.1 0.7 copy-done.14
  9.7 0.7 copy-done.15
  10.4 15.7 %project.1 = (bf16[512,512]{1,0:T(8,128)(2,1)S(1)}, s32[32,128]{1,0:T(8,128)S(1)}, bf16[16,512]{1,0:T(8,128)(2,1)S(1)}, f32[64,128]{1,0:T(8,128)S(1)}, bf16[4096,512]{1,0:T(8,128)(2,1)S(1)}) custom-call(s32[16]{0:T(128)S(1)} %copy-done.14, s32[16]{0:T(128)S(1)} %copy-done.15, bf16[16,2048]{1,0:T(8,128)(2,1)S(1)} %copy-done.9, ...), custom_call_target="tpu_custom_call" | custom-call | tf_op jit(solution)/shard_map/project/pallas_call | solution.py:513
  26.1 0.0 copy-start.1
  26.1 2.0 %copy-done.1 = bf16[4096,512]{1,0:T(8,128)(2,1)} copy-done((bf16[4096,512]{1,0:T(8,128)(2,1)}, bf16[4096,512]{1,0:T(8,128)(2,1)S(1)}, u32[]{:S(2)}) %copy-start.1) | copy-done | bytes 4194328
  28.1 0.0 copy-done.11
  28.1 0.0 copy-done.13
  28.1 2.2 %copy-done.2 = bf16[4096,512]{1,0:T(8,128)(2,1)S(1)} copy-done((bf16[4096,512]{1,0:T(8,128)(2,1)S(1)}, bf16[4096,512]{1,0:T(8,128)(2,1)}, u32[]{:S(2)}) %copy-start.2) | copy-done | bytes 4194328
  30.3 7.7 %attend.1.part_h = bf16[512,640]{1,0:T(8,128)(2,1)S(1)} custom-call(s32[1]{0:T(128)} %bitcast.base_s, bf16[512,512]{1,0:T(8,128)(2,1)S(1)} %get-tuple-element.7.qall, s32[32,128]{1,0:T(8,128)S(1)} %get-tuple-element.8.lens, s32[4,128]{1,0:T(4,128)S(1)} %bitcast.16, s32[32,128]{1,0:T(8,128)S(1)} %bitcast.15, bf16[4096,512]{1,0:T(8,128)(2,1)S(1)} %copy-done.2), custom_call_target="tpu_custom_call" | custom-call | tf_op jit(solution)/shard_map/attend/pallas_call | solution.py:545
  38.0 0.0 copy-done.16
  38.0 0.0 copy-done.6
  38.0 0.0 copy-done.10
  38.0 0.0 copy-start.4
  38.1 2.2 %copy-done.4 = bf16[2048,1024]{1,0:T(8,128)(2,1)S(1)} copy-done((bf16[2048,1024]{1,0:T(8,128)(2,1)S(1)}, bf16[2048,1024]{1,0:T(8,128)(2,1)}, u32[]{:S(2)}) %copy-start.4) | copy-done | bytes 4194328
  40.2 31.8 %finish.1 = f32[16,2048]{1,0:T(8,128)S(1)} custom-call(bf16[512,640]{1,0:T(8,128)(2,1)S(1)} %attend.1.part_h, bf16[16,512]{1,0:T(8,128)(2,1)S(1)} %get-tuple-element.10.qown, f32[64,128]{1,0:T(8,128)S(1)} %get-tuple-element.11.newkv, bf16[16,2048]{1,0:T(8,128)(2,1)S(1)} %copy-done.10, bf16[1,2048]{1,0:T(2,128)(2,1)S(1)} %reshape.37.gain, ...), custom_call_target="tpu_custom_call" | custom-call | tf_op jit(solution)/shard_map/finish/pallas_call | solution.py:562
  72.1 0.7 copy.22
  72.7 0.6 copy.23
  (17 shorter events, 0.0 us)
Async XLA Ops:
  1.3 2.2 %copy-start = (bf16[4096,2,256]{2,1,0:T(2,128)(2,1)S(1)}, bf16[4096,2,256]{2,1,0:T(2,128)(2,1)}, u32[]{:S(2)}) copy-start(bf16[4096,2,256]{2,1,0:T(2,128)(2,1)} %param.21) | copy-start | bytes 12582916
  3.5 1.6 %copy-start.5 = (bf16[2048,512]{1,0:T(8,128)(2,1)S(1)}, bf16[2048,512]{1,0:T(8,128)(2,1)}, u32[]{:S(2)}) copy-start(bf16[2048,512]{1,0:T(8,128)(2,1)} %wq_h.1) | copy-start | bytes 6291460
  5.1 1.2 %copy-start.7 = (bf16[2048,256]{1,0:T(8,128)(2,1)S(1)}, bf16[2048,256]{1,0:T(8,128)(2,1)}, u32[]{:S(2)}) copy-start(bf16[2048,256]{1,0:T(8,128)(2,1)} %wk_h.1) | copy-start | bytes 3145732
  6.3 1.2 %copy-start.8 = (bf16[2048,256]{1,0:T(8,128)(2,1)S(1)}, bf16[2048,256]{1,0:T(8,128)(2,1)}, u32[]{:S(2)}) copy-start(bf16[2048,256]{1,0:T(8,128)(2,1)} %wv_h.1) | copy-start | bytes 3145732
  7.6 0.8 %copy-start.9 = (bf16[16,2048]{1,0:T(8,128)(2,1)S(1)}, bf16[16,2048]{1,0:T(8,128)(2,1)}, u32[]{:S(2)}) copy-start(bf16[16,2048]{1,0:T(8,128)(2,1)} %tok.3) | copy-start | bytes 196612
  8.4 0.7 copy-start.12
  9.1 0.7 copy-start.14
  9.7 0.7 copy-start.15
  10.4 17.7 %copy-start.11 = (s32[4096]{0:T(1024)S(1)}, s32[4096]{0:T(1024)}, u32[]{:S(2)}) copy-start(s32[4096]{0:T(1024)} %param.20) | copy-start | bytes 49156
  10.4 17.7 %copy-start.13 = (s32[512]{0:T(512)S(1)}, s32[512]{0:T(512)}, u32[]{:S(2)}) copy-start(s32[512]{0:T(512)} %param.18) | copy-start | bytes 6148
  10.4 27.6 %copy-start.6 = (bf16[512,2048]{1,0:T(8,128)(2,1)S(1)}, bf16[512,2048]{1,0:T(8,128)(2,1)}, u32[]{:S(2)}) copy-start(bf16[512,2048]{1,0:T(8,128)(2,1)} %wo_h.1) | copy-start | bytes 6291460
  10.4 27.6 %copy-start.10 = (bf16[16,2048]{1,0:T(8,128)(2,1)S(1)}, bf16[16,2048]{1,0:T(8,128)(2,1)}, u32[]{:S(2)}) copy-start(bf16[16,2048]{1,0:T(8,128)(2,1)} %tok.3) | copy-start | bytes 196612
  26.1 2.0 %copy-start.1 = (bf16[4096,512]{1,0:T(8,128)(2,1)}, bf16[4096,512]{1,0:T(8,128)(2,1)S(1)}, u32[]{:S(2)}) copy-start(bf16[4096,512]{1,0:T(8,128)(2,1)S(1)} %get-tuple-element.9.kvd_h) | copy-start | bytes 12582916
  28.1 9.9 %copy-start.16 = (bf16[2048]{0:T(1024)(128)(2,1)S(1)}, bf16[2048]{0:T(1024)(128)(2,1)}, u32[]{:S(2)}) copy-start(bf16[2048]{0:T(1024)(128)(2,1)} %param.27) | copy-start | bytes 12292
  28.1 2.2 %copy-start.2 = (bf16[4096,512]{1,0:T(8,128)(2,1)S(1)}, bf16[4096,512]{1,0:T(8,128)(2,1)}, u32[]{:S(2)}) copy-start(bf16[4096,512]{1,0:T(8,128)(2,1)} %copy-done.1) | copy-start | bytes 12582916
  30.3 7.8 %copy-start.3 = (bf16[2048,1024]{1,0:T(8,128)(2,1)S(1)}, bf16[2048,1024]{1,0:T(8,128)(2,1)}, u32[]{:S(2)}) copy-start(bf16[2048,1024]{1,0:T(8,128)(2,1)} %wg_h.1) | copy-start | bytes 12582916
  38.0 2.2 %copy-start.4 = (bf16[2048,1024]{1,0:T(8,128)(2,1)S(1)}, bf16[2048,1024]{1,0:T(8,128)(2,1)}, u32[]{:S(2)}) copy-start(bf16[2048,1024]{1,0:T(8,128)(2,1)} %wu_h.1) | copy-start | bytes 12582916

commit v2 on v1

--- a/solution.py
+++ b/solution.py
@@ -44,8 +44,10 @@
 
 
 def rms_norm(rows, gain):
-    mean_sq = jnp.mean(rows * rows, axis=-1, keepdims=True)
-    return rows * lax.rsqrt(mean_sq + EPS) * gain.astype(F32)
+    scale = lax.rsqrt(jnp.mean(rows * rows, axis=-1, keepdims=True) + EPS)
+    gain = gain.astype(F32)
+    tiles = [rows[:, i * 128:(i + 1) * 128] * scale * gain[i:i + 1, :] for i in range(gain.shape[0])]
+    return jnp.concatenate(tiles, axis=1).astype(BF16)
 
 
 def frequency_table():
@@ -81,13 +83,19 @@
 
 
 def project_kernel(
-    len_s, pos_s, tok, gain, table, wq_h, wk_h, wv_h, pool_h,
-    qall_o, lens_o, qown_o, newkv_o, kvd_o,
-    wq, wk, wv, pool, kvd, tmp, qall, lens,
-    w_sem, pool_sem, out_sem, ls_sem, lr_sem, lf_sem, qs_sem, qr_sem, fs_sem, fr_sem,
+    len_h, pos_h, tok_h, gain_h, table_h, wq_h, wk_h, wv_h, pool_h,
+    qall, lens, qown_o, newkv_o, kvd,
+    len_s, pos_s, tok, gain, table, wq, wk, wv, pool, tmp,
+    s_sem, w_sem, pool_sem, ls_sem, lr_sem, lf_sem, qs_sem, qr_sem, fs_sem, fr_sem,
 ):
     core, y, z, tp = place()
     chip = y * SIDE + z
+    small = [
+        pltpu.make_async_copy(src, dst, s_sem.at[i])
+        for i, (src, dst) in enumerate(
+            ((len_h, len_s), (pos_h, pos_s), (table_h, table), (tok_h, tok), (gain_h, gain))
+        )
+    ]
     loads = [
         pltpu.make_async_copy(src, dst, w_sem.at[i])
         for i, (src, dst) in enumerate(((wq_h, wq), (wk_h, wk), (wv_h, wv)))
@@ -97,7 +105,7 @@
         pltpu.make_async_copy(pool_h.at[pl.ds(i * piece, piece)], pool.at[pl.ds(i * piece, piece)], pool_sem.at[i])
         for i in range(4)
     ]
-    for copy in loads + pool_loads:
+    for copy in small + loads + pool_loads:
         copy.start()
 
     barrier = pltpu.get_barrier_semaphore()
@@ -106,6 +114,8 @@
     for peer in peers:
         pl.semaphore_signal(barrier, inc=1, device_id=peer, device_id_type=MESH)
 
+    for copy in small:
+        copy.wait()
     lane = lax.broadcasted_iota(jnp.int32, (1, 128), 1)
     mine = jnp.zeros((1, 128), jnp.int32)
     first_lane = lax.rem(chip, 8) * ROWS
@@ -124,7 +134,7 @@
     def rotate(vectors):
         return vectors * cosine + pltpu.roll(vectors, HEAD_DIM // 2, axis=1) * sine
 
-    normed = rms_norm(tok[...].astype(F32), gain[...]).astype(BF16)
+    normed = rms_norm(tok[...].astype(F32), gain[...])
 
     pl.semaphore_wait(barrier, len(peers))
     my_len = lens.at[pl.ds(core * CHIPS + chip, 1)]
@@ -194,7 +204,6 @@
 
     for i in range(4):
         pool_loads[i].wait()
-    outs = []
     order = (1, 3, 4, 12, 2, 8, 5, 7, 13, 15, 6, 14, 9, 11, 10)
     sends = dict(zip((10, 5, 7, 13, 15, 2, 8, 6, 14, 9, 11, 1, 3, 4, 12), q_sends))
     for i in range(16):
@@ -204,32 +213,17 @@
             forwards.append(forward(k))
             forwards[-1].start()
         untangle(i)
-        if i % 4 == 3:
-            rows = pl.ds((i - 3) * 256, 1024)
-            outs.append(pltpu.make_async_copy(kvd.at[rows], kvd_o.at[rows], out_sem.at[i // 4]))
-            outs[-1].start()
     len_forward.wait()
-    lens_o[...] = lens[...]
     for copy in forwards:
         copy.wait()
-    last = pltpu.make_async_copy(qall, qall_o, out_sem.at[4])
-    last.start()
     for copy in q_sends:
         copy.wait_send()
-    for copy in outs:
-        copy.wait()
-    last.wait()
 
 
 def attend_kernel(
-    base_s, qall, lens, order, mask, kvd_h, part,
-    kvd, scores, order_b, first_b, last_b, pooled, kv_sem,
+    base_s, qall, lens, order, mask, kvd, part,
+    scores, order_b, first_b, last_b, pooled,
 ):
-    loads = []
-    for i in range(8):
-        rows = pl.ds(i * 512, 512)
-        loads.append(pltpu.make_async_copy(kvd_h.at[rows], kvd.at[rows], kv_sem.at[i]))
-        loads[-1].start()
     base = base_s[0]
 
     def request_of(n):
@@ -260,8 +254,6 @@
     windows = (high - low + (WIN - 1)) // WIN
 
     pooled[...] = jnp.zeros_like(pooled)
-    for copy in loads:
-        copy.wait()
 
     slot = lax.broadcasted_iota(jnp.int32, (8, 128), 1)
 
@@ -273,6 +265,8 @@
         query = jnp.dot(pick, qall[...], preferred_element_type=F32).astype(BF16)
         first = first_b[pl.ds(at, WIN), :]
         last = last_b[pl.ds(at, WIN), :]
+        chunk_from = jnp.maximum(jnp.min(first), 0) // 512
+        chunk_to = (jnp.minimum(jnp.max(last), SLOTS) + 511) // 512
         first = jnp.concatenate([first, first], axis=0)
         last = jnp.concatenate([last, last], axis=0)
         stats = jnp.zeros((WIN, 128), F32)
@@ -295,7 +289,7 @@
                     peak = jnp.maximum(peak, part_s)
                 return peak
 
-            peak = lax.fori_loop(0, 8, score, jnp.full((2 * WIN, 128), FLOOR, F32))
+            peak = lax.fori_loop(chunk_from, chunk_to, score, jnp.full((2 * WIN, 128), FLOOR, F32))
             peak = jnp.max(peak, axis=1, keepdims=True)
             peak = jnp.where(peak > 0.5 * FLOOR, peak, 0.0)
 
@@ -311,7 +305,7 @@
                 return total, summed
 
             zero = jnp.zeros((2 * WIN, 128), F32)
-            total, summed = lax.fori_loop(0, 8, weigh, (zero, zero))
+            total, summed = lax.fori_loop(chunk_from, chunk_to, weigh, (zero, zero))
             total = jnp.sum(total, axis=1, keepdims=True)
             mean = (summed / jnp.where(total > 0.0, total, 1.0)).astype(BF16)
             for g in range(2):
@@ -346,9 +340,9 @@
 
 
 def finish_kernel(
-    part_h, qown, newkv, tok, gain, wo_h, wg_h, wu_h, wd_h, out,
-    own, came, comb, rx, mix, down, wo, wg, wu, wd,
-    w_sem, own_sem, ps_sem, pr_sem, cs_sem, cr_sem, ms_sem, mr_sem, ds_sem, dr_sem,
+    part, qown, newkv, tok, gain, wo_h, wg_h, wu_h, wd_h, out,
+    came, comb, rx, mix, down, wo, wg, wu, wd,
+    w_sem, ps_sem, pr_sem, cs_sem, cr_sem, ms_sem, mr_sem, ds_sem, dr_sem,
 ):
     core, y, z, tp = place()
     chip = y * SIDE + z
@@ -358,8 +352,6 @@
     beside = [device(chip, core, lax.rem(tp + d, 4)) for d in range(1, 4)]
     for peer in peers + beside:
         pl.semaphore_signal(barrier, inc=1, device_id=peer, device_id_type=MESH)
-    mine = pltpu.make_async_copy(part_h.at[pl.ds(pl.multiple_of(core * HALF, HALF), HALF)], own, own_sem)
-    mine.start()
     pl.semaphore_wait(barrier, len(peers) + len(beside))
 
     def rows_of(dy):
@@ -370,7 +362,7 @@
     for dy in turns:
         swaps.append(
             pltpu.make_async_remote_copy(
-                src_ref=part_h.at[pl.ds(pl.multiple_of((1 - core) * HALF + rows_of(dy), 64), 64)],
+                src_ref=part.at[pl.ds(pl.multiple_of((1 - core) * HALF + rows_of(dy), 64), 64)],
                 dst_ref=came.at[pl.ds(rows_of(dy), 64)],
                 send_sem=ps_sem.at[dy], recv_sem=pr_sem.at[dy], device_id=sibling, device_id_type=MESH,
             )
@@ -383,13 +375,13 @@
     for copy in loads:
         copy.start()
 
-    mine.wait()
     lane64 = lax.broadcasted_iota(jnp.int32, (64, 128), 1)
     sends = []
     for dy, swap in zip(turns, swaps):
         swap.wait_recv()
         rows = pl.ds(rows_of(dy), 64)
-        peak_a, total_a = peaks_totals(own[rows, pl.ds(QW, 128)])
+        mine = pl.ds(pl.multiple_of(core * HALF + rows_of(dy), 64), 64)
+        peak_a, total_a = peaks_totals(part[mine, pl.ds(QW, 128)])
         peak_b, total_b = peaks_totals(came[rows, pl.ds(QW, 128)])
         peak = jnp.maximum(peak_a, peak_b)
         left = total_a * jnp.exp(peak_a - peak)
@@ -399,7 +391,7 @@
         for h in range(4):
             cols = pl.ds(h * HEAD_DIM, HEAD_DIM)
             comb[rows, cols] = (
-                own[rows, cols].astype(F32) * (left * share)[:, h:h + 1]
+                part[mine, cols].astype(F32) * (left * share)[:, h:h + 1]
                 + came[rows, cols].astype(F32) * (right * share)[:, h:h + 1]
             ).astype(BF16)
         stats = jnp.where(lane64 < 4, jnp.where(total > 0.0, peak, 0.0), 0.0)
@@ -482,7 +474,7 @@
     for copy in mixes:
         copy.wait_recv()
     mid = tok[...].astype(F32) + summed_terms(mix)
-    normed = rms_norm(mid, gain[...]).astype(BF16)
+    normed = rms_norm(mid, gain[...])
     loads[1].wait()
     loads[2].wait()
     acts = []
@@ -505,9 +497,12 @@
     tokens, lengths, pool_order, positions, slot_mask, kv_cache, attn_gain,
     w_query, w_key, w_value, w_out, ffn_gain, w_gate, w_up, w_down,
 ):
+    def stay(*arrays):
+        return [pltpu.with_memory_space_constraint(a, pltpu.HBM) for a in arrays]
+
     vmem = pl.BlockSpec(memory_space=pltpu.VMEM)
     smem = pl.BlockSpec(memory_space=pltpu.SMEM)
-    hbm = pl.BlockSpec(memory_space=pl.ANY)
+    hbm = pl.BlockSpec(memory_space=pltpu.HBM)
     dma = pltpu.SemaphoreType.DMA
     pool = kv_cache.reshape(SLOTS, 2, 2, HEAD_DIM).transpose(0, 2, 1, 3).reshape(4 * SLOTS, HEAD_DIM)
     qall, lens, qown, newkv, kvd = pl.pallas_call(
@@ -519,18 +514,20 @@
             jax.ShapeDtypeStruct((4 * ROWS, HEAD_DIM), F32),
             jax.ShapeDtypeStruct((SLOTS, QW), BF16),
         ),
-        in_specs=[smem, smem, vmem, vmem, vmem, hbm, hbm, hbm, hbm],
-        out_specs=(hbm, vmem, vmem, vmem, hbm),
+        in_specs=[hbm] * 9,
+        out_specs=(vmem,) * 5,
         scratch_shapes=[
+            pltpu.SMEM((ROWS,), jnp.int32),
+            pltpu.SMEM((ROWS,), jnp.int32),
+            pltpu.VMEM((ROWS, 2048), BF16),
+            pltpu.VMEM((16, 128), BF16),
+            pltpu.VMEM((8, 128), F32),
             pltpu.VMEM((2048, 512), BF16),
             pltpu.VMEM((2048, 256), BF16),
             pltpu.VMEM((2048, 256), BF16),
             pltpu.VMEM((4 * SLOTS, HEAD_DIM), BF16),
-            pltpu.VMEM((SLOTS, QW), BF16),
             pltpu.VMEM((1024, HEAD_DIM), F32),
-            pltpu.VMEM((REQS, QW), BF16),
-            pltpu.VMEM((32, 128), jnp.int32),
-            dma((3,)), dma((4,)), dma((5,)), dma((16,)), dma((16,)), dma((2,)),
+            dma((5,)), dma((3,)), dma((4,)), dma((16,)), dma((16,)), dma((2,)),
             dma((16,)), dma((16,)), dma((16,)), dma((16,)),
         ],
         compiler_params=pltpu.CompilerParams(
@@ -538,23 +535,23 @@
         ),
         name="project",
     )(
-        lengths, positions, tokens, attn_gain.reshape(1, -1), jnp.asarray(frequency_table()),
-        w_query, w_key, w_value, pool,
+        *stay(
+            lengths, positions, tokens, attn_gain.reshape(16, 128), jnp.asarray(frequency_table()),
+            w_query, w_key, w_value, pool,
+        )
     )
     base = (lax.axis_index("req") * SLOTS).astype(jnp.int32).reshape(1)
     part = pl.pallas_call(
         attend_kernel,
         out_shape=jax.ShapeDtypeStruct((REQS, PW), BF16),
-        in_specs=[smem, vmem, vmem, vmem, vmem, hbm],
+        in_specs=[smem, vmem, vmem, vmem, vmem, vmem],
         out_specs=vmem,
         scratch_shapes=[
-            pltpu.VMEM((SLOTS, QW), BF16),
             pltpu.VMEM((2 * WIN, SLOTS), F32),
             pltpu.VMEM((REQS, 128), jnp.int32),
             pltpu.VMEM((REQS, 128), jnp.int32),
             pltpu.VMEM((REQS, 128), jnp.int32),
             pltpu.VMEM((REQS, PW), BF16),
-            dma((8,)),
         ],
         compiler_params=pltpu.CompilerParams(vmem_limit_bytes=40 << 20),
         name="attend",
@@ -562,10 +559,9 @@
     hidden = pl.pallas_call(
         finish_kernel,
         out_shape=jax.ShapeDtypeStruct((ROWS, 2048), F32),
-        in_specs=[hbm, vmem, vmem, vmem, vmem, hbm, hbm, hbm, hbm],
+        in_specs=[vmem, vmem, vmem, vmem, vmem, hbm, hbm, hbm, hbm],
         out_specs=vmem,
         scratch_shapes=[
-            pltpu.VMEM((HALF, PW), BF16),
             pltpu.VMEM((HALF, PW), BF16),
             pltpu.VMEM((HALF, PW), BF16),
             pltpu.VMEM((CHIPS, ROWS, PW), BF16),
@@ -575,14 +571,14 @@
             pltpu.VMEM((2048, 1024), BF16),
             pltpu.VMEM((2048, 1024), BF16),
             pltpu.VMEM((1024, 2048), BF16),
-            dma((4,)), dma, dma((4,)), dma((4,)), dma((16,)), dma((16,)),
+            dma((4,)), dma((4,)), dma((4,)), dma((16,)), dma((16,)),
             dma((4, 3)), dma((4, 3)), dma((4, 3)), dma((4, 3)),
         ],
         compiler_params=pltpu.CompilerParams(
             collective_id=1, has_side_effects=True, vmem_limit_bytes=40 << 20
         ),
         name="finish",
-    )(part, qown, newkv, tokens, ffn_gain.reshape(1, -1), w_out, w_gate, w_up, w_down)
+    )(part, qown, newkv, tokens, ffn_gain.reshape(16, 128), *stay(w_out, w_gate, w_up, w_down))
     new_kv = newkv.reshape(ROWS, 2, 2, HEAD_DIM).transpose(0, 2, 1, 3).reshape(ROWS, 2, 256)
     return hidden, new_kv
 

time: 73.8 us -> 51.3 us (0.70)
  local copies, waits for them, and re-layouts: 17.4 us -> 1.29 us
  Pallas kernels: 55.2 us -> 49.2 us
    unnamed x36 -> x10, local copies, waits for them, and re-layouts: 16.7 us -> 1.29 us
    pallas_call x1, Pallas kernels: 31.8 us -> 26.4 us  [per_device(): pl.pallas_call(finish_kernel, out_shape=jax.ShapeDtypeStruct((ROWS, 2048)...]
where the time goes in v2:
time: 51.3 us; the launch traced here: 51.2 us
  Pallas kernels  49.2 us (96%)
  local copies, waits for them, and re-layouts  1.29 us (3%)
  between operations  0.73 us (1%)
    pallas_call x1, Pallas kernels, per_device(): pl.pallas_call(finish_kernel, out_shape=jax.ShapeDtypeStruct((ROWS, 2048)...  26.4 us
    pallas_call x1, Pallas kernels, per_device(): pl.pallas_call(project_kernel, out_shape=(jax.ShapeDtypeStruct((REQS, QW)...  15.3 us
    pallas_call x1, Pallas kernels, per_device(): pl.pallas_call(attend_kernel, out_shape=jax.ShapeDtypeStruct((REQS, PW),...  7.53 us
    unnamed x10, local copies, waits for them, and re-layouts  1.29 us

profile of v2, /device:TPU:0, one launch (start us, length us, event | category | flops | bytes accessed | tf_op | source)
XLA Modules:
  0.0 51.2 jit_solution(14481545616869660651)
XLA Ops:
  0.6 0.0 copy-start.1
  0.6 0.0 copy-start.3
  0.7 15.3 %project.1 = (bf16[512,512]{1,0:T(8,128)(2,1)S(1)}, s32[32,128]{1,0:T(8,128)S(1)}, bf16[16,512]{1,0:T(8,128)(2,1)S(1)}, f32[64,128]{1,0:T(8,128)S(1)}, bf16[4096,512]{1,0:T(8,128)(2,1)S(1)}) custom-call(s32[16]{0:T(128)} %len_h.1, s32[16]{0:T(128)} %pos_h.1, bf16[16,2048]{1,0:T(8,128)(2,1)} %tok.1, bf16[16,128]{1,0:T(8,128)(2,1)} %bitcast.20, ...), custom_call_target="tpu_custom_call" | custom-call | tf_op jit(solution)/shard_map/project/pallas_call | solution.py:508
  16.0 0.0 copy-start
  16.0 0.0 copy-start.2
  16.0 0.0 copy-done.1
  16.0 0.0 copy-done.3
  16.0 7.5 %attend.1.part = bf16[512,640]{1,0:T(8,128)(2,1)S(1)} custom-call(s32[1]{0:T(128)} %bitcast.base_s, bf16[512,512]{1,0:T(8,128)(2,1)S(1)} %get-tuple-element.7.qall, s32[32,128]{1,0:T(8,128)S(1)} %get-tuple-element.8.lens, s32[4,128]{1,0:T(4,128)S(1)} %bitcast.18, s32[32,128]{1,0:T(8,128)S(1)} %bitcast.16, bf16[4096,512]{1,0:T(8,128)(2,1)S(1)} %get-tuple-element.9.kvd), custom_call_target="tpu_custom_call" | custom-call | tf_op jit(solution)/shard_map/attend/pallas_call | solution.py:544
  23.6 0.0 copy-done
  23.6 0.0 copy-done.2
  23.6 26.4 %finish.1 = f32[16,2048]{1,0:T(8,128)S(1)} custom-call(bf16[512,640]{1,0:T(8,128)(2,1)S(1)} %attend.1.part, bf16[16,512]{1,0:T(8,128)(2,1)S(1)} %get-tuple-element.10.qown, f32[64,128]{1,0:T(8,128)S(1)} %get-tuple-element.11.newkv, bf16[16,2048]{1,0:T(8,128)(2,1)S(1)} %copy-done, bf16[16,128]{1,0:T(8,128)(2,1)S(1)} %bitcast.17, bf16[512,2048]{1,0:T(8,128)(2,1)} %wo_h.1, ...), custom_call_target="tpu_custom_call" | custom-call | tf_op jit(solution)/shard_map/finish/pallas_call | solution.py:559
  49.9 0.7 %copy.22 = f32[16,2048]{1,0:T(8,128)} copy(f32[16,2048]{1,0:T(8,128)S(1)} %finish.1) | data formatting | bytes 262144
  50.6 0.6 %copy.23 = f32[16,2,256]{2,1,0:T(2,128)} copy(f32[16,2,256]{2,1,0:T(2,128)S(1)} %bitcast.15) | data formatting | bytes 65536
Async XLA Ops:
  0.6 15.4 %copy-start.1 = (s32[4096]{0:T(1024)S(1)}, s32[4096]{0:T(1024)}, u32[]{:S(2)}) copy-start(s32[4096]{0:T(1024)} %param.20) | copy-start | bytes 49156
  0.6 15.4 %copy-start.3 = (s32[512]{0:T(512)S(1)}, s32[512]{0:T(512)}, u32[]{:S(2)}) copy-start(s32[512]{0:T(512)} %param.18) | copy-start | bytes 6148
  16.0 7.6 %copy-start = (bf16[16,2048]{1,0:T(8,128)(2,1)S(1)}, bf16[16,2048]{1,0:T(8,128)(2,1)}, u32[]{:S(2)}) copy-start(bf16[16,2048]{1,0:T(8,128)(2,1)} %tok.1) | copy-start | bytes 196612
  16.0 7.6 %copy-start.2 = (bf16[2048]{0:T(1024)(128)(2,1)S(1)}, bf16[2048]{0:T(1024)(128)(2,1)}, u32[]{:S(2)}) copy-start(bf16[2048]{0:T(1024)(128)(2,1)} %param.27) | copy-start | bytes 12292

commit v3 on v2

v3 whole, which is shorter than its diff:
```python
import functools
import math

import jax
import jax.numpy as jnp
import numpy as np
from jax import lax
from jax.experimental import pallas as pl
from jax.experimental.pallas import tpu as pltpu
from jax.sharding import PartitionSpec as P

MESH = pl.DeviceIdType.MESH
HEAD_DIM = 128
ROPE_BASE = 1000000.0
EPS = 1e-05
FLOOR = -1e30
SCALE = 1.0 / math.sqrt(HEAD_DIM)
SIDE = 4
CHIPS = SIDE * SIDE
ROWS = 16
REQS = 512
SLOTS = 4096
HALF = REQS // 2
QW = 512
PW = QW + 128
WIN = 64
CHUNK = 2048
LOG2E = 1.4426950408889634
BF16 = jnp.bfloat16
F32 = jnp.float32


def place():
    me = lax.axis_index("req")
    core = lax.rem(me, 2)
    chip = me // 2
    return core, chip // SIDE, lax.rem(chip, SIDE), lax.axis_index("tp")


def chip_at(y, z, k):
    return lax.rem(y + k // SIDE, SIDE) * SIDE + lax.rem(z + k % SIDE, SIDE)


def device(chip, core, tp):
    return {"req": chip * 2 + core, "tp": tp}


def rms_norm(rows, gain):
    scale = lax.rsqrt(jnp.mean(rows * rows, axis=-1, keepdims=True) + EPS)
    gain = gain.astype(F32)
    tiles = [rows[:, i * 128:(i + 1) * 128] * scale * gain[i:i + 1, :] for i in range(gain.shape[0])]
    return jnp.concatenate(tiles, axis=1).astype(BF16)


def frequency_table():
    half = HEAD_DIM // 2
    turns = ROPE_BASE ** (-(np.arange(half, dtype=np.float64) * 2.0) / HEAD_DIM) / (2.0 * np.pi)
    first = np.round(turns * 2.0**12) / 2.0**12
    second = np.round((turns - first) * 2.0**23) / 2.0**23
    third = turns - first - second
    table = np.zeros((8, HEAD_DIM), np.float64)
    for i, term in enumerate((first, second, third)):
        table[i] = np.concatenate([term, term])
    return table.astype(np.float32)


def cos_sin(where, table):
    turn = where * table[0:1, :]
    turn = turn - jnp.floor(turn + 0.5)
    turn = turn + where * table[1:2, :]
    turn = turn - jnp.floor(turn + 0.5)
    turn = turn + where * table[2:3, :]
    quarter = jnp.floor(turn * 4.0 + 0.5)
    x = (turn - quarter * 0.25) * np.float32(2.0 * np.pi)
    sq = x * x
    sine = x * (1.0 + sq * (-1.0 / 6 + sq * (1.0 / 120 + sq * (-1.0 / 5040 + sq * (1.0 / 362880)))))
    cosine = 1.0 + sq * (
        -0.5 + sq * (1.0 / 24 + sq * (-1.0 / 720 + sq * (1.0 / 40320 + sq * (-1.0 / 3628800))))
    )
    odd = (quarter == 1.0) | (quarter == -1.0)
    far = (quarter == 2.0) | (quarter == -2.0)
    c = jnp.where(odd, -quarter * sine, jnp.where(far, -cosine, cosine))
    s = jnp.where(odd, quarter * cosine, jnp.where(far, -sine, sine))
    return c, s


def project_kernel(
    len_h, pos_h, tok_h, gain_h, table_h, wq_h, wk_h, wv_h, pool_h,
    qall, qown_o, newkv_o, kvd,
    len_s, pos_s, tok, gain, table, wq, wk, wv, pool, tmp,
    s_sem, w_sem, pool_sem, qs_sem, qr_sem, fs_sem, fr_sem,
):
    core, y, z, tp = place()
    chip = y * SIDE + z
    small = [
        pltpu.make_async_copy(src, dst, s_sem.at[i])
        for i, (src, dst) in enumerate(
            ((len_h, len_s), (pos_h, pos_s), (table_h, table), (tok_h, tok), (gain_h, gain))
        )
    ]
    loads = [
        pltpu.make_async_copy(src, dst, w_sem.at[i])
        for i, (src, dst) in enumerate(((wq_h, wq), (wk_h, wk), (wv_h, wv)))
    ]
    piece = 4 * SLOTS // 4
    pool_loads = [
        pltpu.make_async_copy(pool_h.at[pl.ds(i * piece, piece)], pool.at[pl.ds(i * piece, piece)], pool_sem.at[i])
        for i in range(4)
    ]
    for copy in small + loads + pool_loads:
        copy.start()

    barrier = pltpu.get_barrier_semaphore()
    sibling = device(chip, 1 - core, tp)
    peers = [sibling] + [device(chip_at(y, z, k), core, tp) for k in range(1, CHIPS)]
    for peer in peers:
        pl.semaphore_signal(barrier, inc=1, device_id=peer, device_id_type=MESH)

    for copy in small:
        copy.wait()
    row = lax.broadcasted_iota(jnp.int32, (ROWS, 128), 0)
    lane = lax.broadcasted_iota(jnp.int32, (ROWS, 128), 1)
    where = jnp.zeros((ROWS, 128), jnp.int32)
    digits = jnp.zeros((ROWS, 128), jnp.int32)
    for i in range(ROWS):
        where = jnp.where(row == i, pos_s[i], where)
        digits = jnp.where(row == i, len_s[i], digits)
    digits = jnp.where(lane == 0, digits >> 7, jnp.where(lane == 1, digits & 127, 0)).astype(F32).astype(BF16)
    cosine, sine = cos_sin(where.astype(F32), table[...])
    sine = jnp.where(lane < HEAD_DIM // 2, -sine, sine)

    def rotate(vectors):
        return vectors * cosine + pltpu.roll(vectors, HEAD_DIM // 2, axis=1) * sine

    normed = rms_norm(tok[...].astype(F32), gain[...])

    pl.semaphore_wait(barrier, len(peers))
    loads[0].wait()
    query = jnp.dot(normed, wq[...], preferred_element_type=F32)
    mine_at = pl.multiple_of(core * HALF + chip * ROWS, ROWS)
    for h in range(QW // HEAD_DIM):
        cols = pl.ds(h * HEAD_DIM, HEAD_DIM)
        turned = rotate(query[:, h * HEAD_DIM:(h + 1) * HEAD_DIM]).astype(BF16)
        qall[pl.ds(mine_at, ROWS), cols] = turned
        qown_o[:, cols] = turned
    qall[pl.ds(mine_at, ROWS), pl.ds(QW, 128)] = digits
    my_rows = qall.at[pl.ds(mine_at, ROWS)]
    q_sends = {}
    for k in range(1, CHIPS):
        q_sends[k] = pltpu.make_async_remote_copy(
            src_ref=my_rows, dst_ref=my_rows, send_sem=qs_sem.at[k], recv_sem=qr_sem.at[k],
            device_id=peers[k], device_id_type=MESH,
        )
    far_first = (10, 9, 11, 8, 6, 5, 7, 4, 14, 13, 15, 12, 2, 1, 3)
    for k in far_first:
        q_sends[k].start()

    def forward(dy):
        source = lax.rem(y + SIDE - dy, SIDE) * SIDE * ROWS
        rows = qall.at[pl.ds(pl.multiple_of(core * HALF + source, SIDE * ROWS), SIDE * ROWS)]
        return pltpu.make_async_remote_copy(
            src_ref=rows, dst_ref=rows, send_sem=fs_sem.at[dy], recv_sem=fr_sem.at[dy],
            device_id=sibling, device_id_type=MESH,
        )

    loads[1].wait()
    key = jnp.dot(normed, wk[...], preferred_element_type=F32)
    loads[2].wait()
    value = jnp.dot(normed, wv[...], preferred_element_type=F32)
    for h in range(2):
        cols = slice(h * HEAD_DIM, (h + 1) * HEAD_DIM)
        newkv_o[pl.ds(2 * h, ROWS, stride=4), :] = rotate(key[:, cols])
        newkv_o[pl.ds(2 * h + 1, ROWS, stride=4), :] = value[:, cols]

    def untangle(i):
        tmp[...] = pool[pl.ds(i * 1024, 1024), :].astype(F32)
        for j in range(4):
            kvd[pl.ds(i * 256, 256), pl.ds(j * 128, 128)] = tmp[pl.ds(j, 256, stride=4), :].astype(BF16)

    for i in range(4):
        pool_loads[i].wait()
    forwards = []
    for i, dy in enumerate((2, 1, 3, 0)):
        for j in range(SIDE):
            untangle(4 * i + j)
        for dz in range(SIDE):
            if dy or dz:
                q_sends[dy * SIDE + dz].wait_recv()
        forwards.append(forward(dy))
        forwards[-1].start()
    for copy in forwards:
        copy.wait()
    for copy in q_sends.values():
        copy.wait_send()


def request_of(n):
    return ((n >> 4) & 15) * 32 + (n >> 8) * 16 + (n & 15)


def as_bf16(flags):
    return flags.astype(F32).astype(BF16)


def attend_kernel(
    base_s, qall, order, mask, kvd, newkv, pooled, newkv_o,
    scores, order_b, first_b, last_b, out_sem,
):
    leave = pltpu.make_async_copy(newkv, newkv_o, out_sem)
    leave.start()
    base = base_s[0]

    n_lane = [request_of(lax.broadcasted_iota(jnp.int32, (1, 128), 1) + 128 * t) for t in range(4)]
    for t in range(4):
        tile = jnp.broadcast_to(order[t:t + 1, :], (128, 128)).astype(F32)
        order_b[pl.ds(128 * t, 128), :] = jnp.transpose(tile).astype(jnp.int32)
    p_sub = lax.broadcasted_iota(jnp.int32, (REQS, 128), 0)
    here, upto = [], []
    for t in range(4):
        match = order_b[...] == n_lane[t]
        pos = jnp.sum(jnp.where(match, p_sub.astype(F32), 0.0), axis=0, keepdims=True).astype(jnp.int32)
        here.append(as_bf16(match))
        upto.append(as_bf16(pos <= p_sub))
    digits = qall[:, pl.ds(QW, 128)]

    def lengths_by(flags):
        found = jnp.dot(jnp.concatenate(flags, axis=1), digits, preferred_element_type=F32)
        return (found[:, 0:1] * 128.0 + found[:, 1:2]).astype(jnp.int32)

    ends = lengths_by(upto) - base
    starts = ends - lengths_by(here)
    first_b[...] = jnp.broadcast_to(starts, (REQS, 128))
    last_b[...] = jnp.broadcast_to(ends, (REQS, 128))
    low = jnp.sum((ends <= 0).astype(jnp.int32))
    high = jnp.sum((starts < SLOTS).astype(jnp.int32))
    low = (low // 16) * 16
    windows = (high - low + (WIN - 1)) // WIN

    pooled[...] = jnp.zeros_like(pooled)
    slot = lax.broadcasted_iota(jnp.int32, (1, 128), 1)
    ones = jnp.ones((CHUNK, 128), BF16)

    @pl.loop(0, windows)
    def _(w):
        at = pl.multiple_of(jnp.minimum(low + w * WIN, REQS - WIN), 16)
        own = order_b[pl.ds(at, WIN), :]
        pick = jnp.concatenate([as_bf16(own == n_lane[t]) for t in range(4)], axis=1)
        query = jnp.dot(pick, qall[:, pl.ds(0, QW)], preferred_element_type=F32).astype(BF16)
        first = first_b[pl.ds(at, WIN), :]
        last = last_b[pl.ds(at, WIN), :]
        chunk_from = jnp.maximum(jnp.min(first), 0) // CHUNK
        chunk_to = (jnp.minimum(jnp.max(last), SLOTS) + (CHUNK - 1)) // CHUNK
        first = jnp.concatenate([first, first], axis=0)
        last = jnp.concatenate([last, last], axis=0)
        rows = [jnp.concatenate([head(query, 2 * j), head(query, 2 * j + 1)], axis=0) for j in range(2)]

        def score(c, peaks):
            start = pl.multiple_of(c * CHUNK, CHUNK)
            s = [
                lax.dot_general(
                    rows[j], kvd[pl.ds(start, CHUNK), pl.ds(2 * j * 128, 128)],
                    (((1,), (1,)), ((), ())), preferred_element_type=F32,
                )
                for j in range(2)
            ]
            peaks = list(peaks)
            for i in range(CHUNK // 128):
                live = mask[pl.ds(c * (CHUNK // 128) + i, 1), :] == 1
                index = jnp.where(live, slot + (start + i * 128), -REQS * 8192)
                ok = (index >= first) & (index < last)
                for j in range(2):
                    found = jnp.where(ok, s[j][:, i * 128:(i + 1) * 128], FLOOR)
                    scores[j, :, pl.ds(pl.multiple_of(start + i * 128, 128), 128)] = found
                    peaks[j] = jnp.maximum(peaks[j], found)
            return tuple(peaks)

        least = jnp.full((2 * WIN, 128), FLOOR, F32)
        peaks = lax.fori_loop(chunk_from, chunk_to, score, (least, least))
        peaks = [jnp.max(peak, axis=1, keepdims=True) for peak in peaks]
        peaks = [jnp.where(peak > 0.5 * FLOOR, peak, 0.0) for peak in peaks]

        def weigh(c, sums):
            start = pl.multiple_of(c * CHUNK, CHUNK)
            out = []
            for j in range(2):
                weight = jnp.exp2((scores[j, :, pl.ds(start, CHUNK)] - peaks[j]) * (SCALE * LOG2E)).astype(BF16)
                values = kvd[pl.ds(start, CHUNK), pl.ds((2 * j + 1) * 128, 128)]
                both = jnp.concatenate([values, ones], axis=1)
                out.append(sums[j] + jnp.dot(weight, both, preferred_element_type=F32))
            return tuple(out)

        zero = jnp.zeros((2 * WIN, 256), F32)
        sums = lax.fori_loop(chunk_from, chunk_to, weigh, (zero, zero))
        top, totals = [], []
        for j in range(2):
            total = sums[j][:, 128:]
            mean = (sums[j][:, :128] / jnp.where(total > 0.0, total, 1.0)).astype(BF16)
            for g in range(2):
                h, part_rows = 2 * j + g, slice(g * WIN, (g + 1) * WIN)
                pooled[pl.ds(at, WIN), pl.ds(h * HEAD_DIM, HEAD_DIM)] = mean[part_rows]
                top.append(jnp.broadcast_to(peaks[j][part_rows] * SCALE, (WIN, 128)))
                totals.append(total[part_rows])
        pooled[pl.ds(at, WIN), pl.ds(QW, 128)] = stats_of(top, totals)

    leave.wait()


def pack_stats(stats):
    lane = lax.broadcasted_iota(jnp.int32, stats.shape, 1)
    top = stats.astype(BF16).astype(F32)
    rest = stats - top
    middle = rest.astype(BF16).astype(F32)
    rest = rest - middle
    kept = jnp.where(lane < 8, top, jnp.where(lane < 16, middle, jnp.where(lane < 24, rest, 0.0)))
    return kept.astype(BF16)


def stats_of(peaks, totals):
    value = lax.broadcasted_iota(jnp.int32, peaks[0].shape, 1) & 7
    stats = jnp.zeros(peaks[0].shape, F32)
    for h in range(4):
        stats = jnp.where(value == h, peaks[h], stats)
        stats = jnp.where(value == 4 + h, totals[h], stats)
    return pack_stats(stats)


def spreader():
    value = lax.broadcasted_iota(jnp.int32, (128, 2 * QW), 0)
    column = lax.broadcasted_iota(jnp.int32, (128, 2 * QW), 1)
    return ((value < 24) & ((value & 7) == (column >> 7))).astype(F32).astype(BF16)


def head(block, h):
    return block[:, h * HEAD_DIM:(h + 1) * HEAD_DIM]


def finish_kernel(
    pooled, order, qown, newkv, tok, gain, wo_h, wg_h, wu_h, wd_h, out,
    part, came, comb, rx, mix, down, spread, left_stats, right_stats, wo, wg, wu, wd,
    w_sem, p_sem, cs_sem, cr_sem, ms_sem, mr_sem, ds_sem, dr_sem,
):
    core, y, z, tp = place()
    chip = y * SIDE + z
    barrier = pltpu.get_barrier_semaphore()
    sibling = device(chip, 1 - core, tp)
    peers = [sibling] + [device(chip_at(y, z, k), core, tp) for k in range(1, CHIPS)]
    beside = [device(chip, core, lax.rem(tp + d, 4)) for d in range(1, 4)]
    for peer in peers + beside:
        pl.semaphore_signal(barrier, inc=1, device_id=peer, device_id_type=MESH)
    loads = [
        pltpu.make_async_copy(src, dst, w_sem.at[i])
        for i, (src, dst) in enumerate(((wo_h, wo), (wg_h, wg), (wu_h, wu), (wd_h, wd)))
    ]
    for copy in loads:
        copy.start()
    n_sub = request_of(lax.broadcasted_iota(jnp.int32, (REQS, 128), 0))
    place_n = jnp.concatenate([as_bf16(order[t:t + 1, :] == n_sub) for t in range(4)], axis=1)
    part[...] = jnp.dot(place_n, pooled[...], preferred_element_type=F32).astype(BF16)
    spread[...] = spreader()
    half = pl.multiple_of(core * HALF, HALF)
    left_stats[...] = jnp.dot(part[pl.ds(half, HALF), pl.ds(QW, 128)], spread[...], preferred_element_type=F32)
    own_peaks, own_values = [], []
    for h in range(4):
        keys = newkv[pl.ds(2 * (h // 2), ROWS, stride=4), :].astype(BF16).astype(F32)
        query = head(qown[...], h).astype(F32)
        score = jnp.sum(query * keys, axis=1, keepdims=True) * SCALE
        own_peaks.append(jnp.broadcast_to(score, (ROWS, HEAD_DIM)))
        own_values.append(newkv[pl.ds(2 * (h // 2) + 1, ROWS, stride=4), :].astype(BF16).astype(F32))
    pl.semaphore_wait(barrier, len(peers) + len(beside))

    def rows_of(dy):
        return pl.multiple_of(lax.rem(y + dy, SIDE) * 64, 64)

    turns = (2, 1, 3, 0)
    swap = pltpu.make_async_remote_copy(
        src_ref=part.at[pl.ds(pl.multiple_of(HALF - half, HALF), HALF)], dst_ref=came,
        send_sem=p_sem.at[0], recv_sem=p_sem.at[1], device_id=sibling, device_id_type=MESH,
    )
    swap.start()
    swap.wait_recv()
    right_stats[...] = jnp.dot(came[:, pl.ds(QW, 128)], spread[...], preferred_element_type=F32)

    def stat(ref, rows, h):
        totals = ref[rows, pl.ds(QW + h * HEAD_DIM, HEAD_DIM)]
        return jnp.where(totals > 0.0, ref[rows, pl.ds(h * HEAD_DIM, HEAD_DIM)], FLOOR), totals

    sends = []
    for dy in turns:
        rows = pl.ds(rows_of(dy), 64)
        mine = pl.ds(pl.multiple_of(half + rows_of(dy), 64), 64)
        peaks, totals = [], []
        for h in range(4):
            cols = pl.ds(h * HEAD_DIM, HEAD_DIM)
            peak_a, total_a = stat(left_stats, rows, h)
            peak_b, total_b = stat(right_stats, rows, h)
            peak = jnp.maximum(peak_a, peak_b)
            left = total_a * jnp.exp(peak_a - peak)
            right = total_b * jnp.exp(peak_b - peak)
            total = left + right
            summed = part[mine, cols].astype(F32) * left + came[rows, cols].astype(F32) * right
            comb[rows, cols] = (summed / jnp.where(total > 0.0, total, 1.0)).astype(BF16)
            peaks.append(jnp.where(total > 0.0, peak, 0.0))
            totals.append(total)
        comb[rows, pl.ds(QW, 128)] = stats_of(peaks, totals)
        for dz in (2, 1, 3, 0):
            k = dy * SIDE + dz
            if k == 0:
                continue
            block = comb.at[pl.ds(pl.multiple_of(chip_at(y, z, k) * ROWS, ROWS), ROWS)]
            sends.append(
                pltpu.make_async_remote_copy(
                    src_ref=block, dst_ref=rx.at[k], send_sem=cs_sem.at[k], recv_sem=cr_sem.at[k],
                    device_id=peers[k], device_id_type=MESH,
                )
            )
            sends[-1].start()
    rx[0] = comb[pl.ds(pl.multiple_of(chip * ROWS, ROWS), ROWS), :]

    for copy in sends:
        copy.wait_recv()
    found = [rx[k, :, pl.ds(QW, 128)] for k in range(CHIPS)]
    left_stats[...] = jnp.dot(jnp.concatenate(found, axis=0), spread[...], preferred_element_type=F32)
    context = []
    for h in range(4):
        cols = pl.ds(h * HEAD_DIM, HEAD_DIM)
        stats = [stat(left_stats, pl.ds(k * ROWS, ROWS), h) for k in range(CHIPS)]
        peak = own_peaks[h]
        for other, _ in stats:
            peak = jnp.maximum(peak, other)
        total = jnp.exp(own_peaks[h] - peak)
        summed = total * own_values[h]
        for k in range(CHIPS):
            weight = stats[k][1] * jnp.exp(stats[k][0] - peak)
            total = total + weight
            summed = summed + weight * rx[k, :, cols].astype(F32)
        context.append((summed / total).astype(BF16))
    context = jnp.concatenate(context, axis=1)

    def over_tp(left, right, width, terms, send, recv):
        copies = []
        for n in range(4):
            cols = pl.ds(n * width, width)
            terms[tp, :, cols] = jnp.dot(left, right[:, cols], preferred_element_type=F32).astype(BF16)
            for d in range(3):
                ref = terms.at[tp, :, cols]
                copies.append(
                    pltpu.make_async_remote_copy(
                        src_ref=ref, dst_ref=ref, send_sem=send.at[n, d], recv_sem=recv.at[n, d],
                        device_id=beside[d], device_id_type=MESH,
                    )
                )
                copies[-1].start()
        return copies

    def summed_terms(terms):
        total = terms[0].astype(F32)
        for t in range(1, 4):
            total = total + terms[t].astype(F32)
        return total

    loads[0].wait()
    mixes = over_tp(context, wo, 512, mix, ms_sem, mr_sem)
    for copy in mixes:
        copy.wait_recv()
    mid = tok[...].astype(F32) + summed_terms(mix)
    normed = rms_norm(mid, gain[...])
    loads[1].wait()
    loads[2].wait()
    acts = []
    for n in range(2):
        cols = pl.ds(n * 512, 512)
        gate = jnp.dot(normed, wg[:, cols], preferred_element_type=F32)
        upper = jnp.dot(normed, wu[:, cols], preferred_element_type=F32)
        acts.append((gate / (1.0 + jnp.exp(-gate)) * upper).astype(BF16))
    act = jnp.concatenate(acts, axis=1)
    loads[3].wait()
    downs = over_tp(act, wd, 512, down, ds_sem, dr_sem)
    for copy in downs:
        copy.wait_recv()
    out[...] = mid + summed_terms(down)
    for copy in [swap] + sends + mixes + downs:
        copy.wait_send()


def per_device(
    tokens, lengths, pool_order, positions, slot_mask, kv_cache, attn_gain,
    w_query, w_key, w_value, w_out, ffn_gain, w_gate, w_up, w_down,
):
    def stay(*arrays):
        return [pltpu.with_memory_space_constraint(a, pltpu.HBM) for a in arrays]

    vmem = pl.BlockSpec(memory_space=pltpu.VMEM)
    smem = pl.BlockSpec(memory_space=pltpu.SMEM)
    hbm = pl.BlockSpec(memory_space=pltpu.HBM)
    dma = pltpu.SemaphoreType.DMA
    pool = kv_cache.reshape(SLOTS, 2, 2, HEAD_DIM).transpose(0, 2, 1, 3).reshape(4 * SLOTS, HEAD_DIM)
    qall, qown, newkv, kvd = pl.pallas_call(
        project_kernel,
        out_shape=(
            jax.ShapeDtypeStruct((REQS, PW), BF16),
            jax.ShapeDtypeStruct((ROWS, QW), BF16),
            jax.ShapeDtypeStruct((4 * ROWS, HEAD_DIM), F32),
            jax.ShapeDtypeStruct((SLOTS, QW), BF16),
        ),
        in_specs=[hbm] * 9,
        out_specs=(vmem,) * 4,
        scratch_shapes=[
            pltpu.SMEM((ROWS,), jnp.int32),
            pltpu.SMEM((ROWS,), jnp.int32),
            pltpu.VMEM((ROWS, 2048), BF16),
            pltpu.VMEM((16, 128), BF16),
            pltpu.VMEM((8, 128), F32),
            pltpu.VMEM((2048, 512), BF16),
            pltpu.VMEM((2048, 256), BF16),
            pltpu.VMEM((2048, 256), BF16),
            pltpu.VMEM((4 * SLOTS, HEAD_DIM), BF16),
            pltpu.VMEM((1024, HEAD_DIM), F32),
            dma((5,)), dma((3,)), dma((4,)), dma((16,)), dma((16,)), dma((4,)), dma((4,)),
        ],
        compiler_params=pltpu.CompilerParams(
            collective_id=0, has_side_effects=True, vmem_limit_bytes=40 << 20
        ),
        name="project",
    )(
        *stay(
            lengths, positions, tokens, attn_gain.reshape(16, 128), jnp.asarray(frequency_table()),
            w_query, w_key, w_value, pool,
        )
    )
    base = (lax.axis_index("req") * SLOTS).astype(jnp.int32).reshape(1)
    part, new_kv = pl.pallas_call(
        attend_kernel,
        out_shape=(
            jax.ShapeDtypeStruct((REQS, PW), BF16),
            pltpu.HBM((4 * ROWS, HEAD_DIM), F32),
        ),
        in_specs=[smem, vmem, vmem, vmem, vmem, vmem],
        out_specs=(vmem, hbm),
        scratch_shapes=[
            pltpu.VMEM((2, 2 * WIN, SLOTS), F32),
            pltpu.VMEM((REQS, 128), jnp.int32),
            pltpu.VMEM((REQS, 128), jnp.int32),
            pltpu.VMEM((REQS, 128), jnp.int32),
            dma,
        ],
        compiler_params=pltpu.CompilerParams(vmem_limit_bytes=40 << 20),
        name="attend",
    )(base, qall, pool_order.reshape(4, 128), slot_mask.reshape(32, 128), kvd, newkv)
    hidden = pl.pallas_call(
        finish_kernel,
        out_shape=jax.ShapeDtypeStruct((ROWS, 2048), F32),
        in_specs=[vmem] * 6 + [hbm] * 4,
        out_specs=vmem,
        scratch_shapes=[
            pltpu.VMEM((REQS, PW), BF16),
            pltpu.VMEM((HALF, PW), BF16),
            pltpu.VMEM((HALF, PW), BF16),
            pltpu.VMEM((CHIPS, ROWS, PW), BF16),
            pltpu.VMEM((4, ROWS, 2048), BF16),
            pltpu.VMEM((4, ROWS, 2048), BF16),
            pltpu.VMEM((128, 2 * QW), BF16),
            pltpu.VMEM((HALF, 2 * QW), F32),
            pltpu.VMEM((HALF, 2 * QW), F32),
            pltpu.VMEM((512, 2048), BF16),
            pltpu.VMEM((2048, 1024), BF16),
            pltpu.VMEM((2048, 1024), BF16),
            pltpu.VMEM((1024, 2048), BF16),
            dma((4,)), dma((2,)), dma((16,)), dma((16,)),
            dma((4, 3)), dma((4, 3)), dma((4, 3)), dma((4, 3)),
        ],
        compiler_params=pltpu.CompilerParams(
            collective_id=1, has_side_effects=True, vmem_limit_bytes=40 << 20
        ),
        name="finish",
    )(part, pool_order.reshape(4, 128), qown, newkv, tokens, ffn_gain.reshape(16, 128), *stay(w_out, w_gate, w_up, w_down))
    new_kv = new_kv.reshape(ROWS, 2, 2, HEAD_DIM).transpose(0, 2, 1, 3).reshape(ROWS, 2, 256)
    return hidden, new_kv


def solution(mesh):
    placed = (
        P("req", None), P("req"), P(), P("req"), P("req"), P("req", None, "tp"), P(),
        P(None, "tp"), P(None, "tp"), P(None, "tp"), P("tp", None), P(),
        P(None, "tp"), P(None, "tp"), P("tp", None),
    )
    return jax.shard_map(
        per_device,
        mesh=mesh,
        in_specs=placed,
        out_specs=(P("req", None), P("req", None, "tp")),
        check_vma=False,
    )
```

time: 51.3 us -> 45.8 us (0.89)
  Pallas kernels: 49.2 us -> 44.3 us
  local copies, waits for them, and re-layouts: 1.29 us -> 0.68 us
    pallas_call x2, Pallas kernels: 22.8 us -> 19.1 us  [the longest x1 15.5 us: per_device(): pl.pallas_call(project_kernel, out_shape=(jax.ShapeDtypeStruct((REQS, PW)...]
    pallas_call x1, Pallas kernels: 26.4 us -> 25.2 us  [per_device(): pl.pallas_call(finish_kernel, out_shape=jax.ShapeDtypeStruct((ROWS, 2048)...]
    unnamed x10 -> x9, local copies, waits for them, and re-layouts: 1.29 us -> 0.68 us
where the time goes in v3:
time: 45.8 us; the launch traced here: 45.7 us
  Pallas kernels  44.3 us (97%)
  between operations  0.73 us (2%)
  local copies, waits for them, and re-layouts  0.68 us (1%)
    pallas_call x1, Pallas kernels, per_device(): pl.pallas_call(finish_kernel, out_shape=jax.ShapeDtypeStruct((ROWS, 2048)...  25.2 us
    pallas_call x1, Pallas kernels, per_device(): pl.pallas_call(project_kernel, out_shape=(jax.ShapeDtypeStruct((REQS, PW)...  15.5 us
    pallas_call x1, Pallas kernels, per_device(): pl.pallas_call(attend_kernel, out_shape=(jax.ShapeDtypeStruct((REQS, PW),...  3.62 us

profile of v3, /device:TPU:0, one launch (start us, length us, event | category | flops | bytes accessed | tf_op | source)
XLA Modules:
  0.0 45.7 jit_solution(9341197905863173462)
XLA Ops:
  0.6 0.0 copy-start.1
  0.6 0.0 copy-start.2
  0.7 15.5 %project.1 = (bf16[512,640]{1,0:T(8,128)(2,1)S(1)}, bf16[16,512]{1,0:T(8,128)(2,1)S(1)}, f32[64,128]{1,0:T(8,128)S(1)}, bf16[4096,512]{1,0:T(8,128)(2,1)S(1)}) custom-call(s32[16]{0:T(128)} %len_h.1, s32[16]{0:T(128)} %pos_h.1, bf16[16,2048]{1,0:T(8,128)(2,1)} %tok.1, bf16[16,128]{1,0:T(8,128)(2,1)} %bitcast.20, f32[8,128]{1,0:T(8,128)} %constant.10.clone.table_h, ...), custom_call_target="tpu_custom_call" | custom-call | tf_op jit(solution)/shard_map/project/pallas_call | solution.py:497
  16.1 0.0 copy-start
  16.1 0.0 copy-start.3
  16.2 0.0 copy-done.1
  16.2 0.0 copy-done.2
  16.2 3.6 %attend.1 = (bf16[512,640]{1,0:T(8,128)(2,1)S(1)}, f32[64,128]{1,0:T(8,128)}) custom-call(s32[1]{0:T(128)} %bitcast.base_s, bf16[512,640]{1,0:T(8,128)(2,1)S(1)} %get-tuple-element.8.qall, s32[4,128]{1,0:T(4,128)S(1)} %bitcast.16, s32[32,128]{1,0:T(8,128)S(1)} %bitcast.15, bf16[4096,512]{1,0:T(8,128)(2,1)S(1)} %get-tuple-element.9.kvd, ...), custom_call_target="tpu_custom_call" | custom-call | tf_op jit(solution)/shard_map/attend/pallas_call | solution.py:531
  19.8 0.0 copy-done
  19.8 0.0 copy-done.3
  19.8 25.2 %finish.1 = f32[16,2048]{1,0:T(8,128)S(1)} custom-call(bf16[512,640]{1,0:T(8,128)(2,1)S(1)} %get-tuple-element.11.pooled, s32[4,128]{1,0:T(4,128)S(1)} %bitcast.17, bf16[16,512]{1,0:T(8,128)(2,1)S(1)} %get-tuple-element.12.qown, f32[64,128]{1,0:T(8,128)S(1)} %get-tuple-element.10.newkv, bf16[16,2048]{1,0:T(8,128)(2,1)S(1)} %copy-done, ...), custom_call_target="tpu_custom_call" | custom-call | tf_op jit(solution)/shard_map/finish/pallas_call | solution.py:549
  45.1 0.7 %copy.21 = f32[16,2048]{1,0:T(8,128)} copy(f32[16,2048]{1,0:T(8,128)S(1)} %finish.1) | data formatting | bytes 262144
Async XLA Ops:
  0.6 15.5 %copy-start.1 = (s32[4096]{0:T(1024)S(1)}, s32[4096]{0:T(1024)}, u32[]{:S(2)}) copy-start(s32[4096]{0:T(1024)} %param.20) | copy-start | bytes 49156
  0.6 15.5 %copy-start.2 = (s32[512]{0:T(512)S(1)}, s32[512]{0:T(512)}, u32[]{:S(2)}) copy-start(s32[512]{0:T(512)} %param.18) | copy-start | bytes 6148
  16.1 3.7 %copy-start = (bf16[16,2048]{1,0:T(8,128)(2,1)S(1)}, bf16[16,2048]{1,0:T(8,128)(2,1)}, u32[]{:S(2)}) copy-start(bf16[16,2048]{1,0:T(8,128)(2,1)} %tok.1) | copy-start | bytes 196612
  16.1 3.7 %copy-start.3 = (bf16[2048]{0:T(1024)(128)(2,1)S(1)}, bf16[2048]{0:T(1024)(128)(2,1)}, u32[]{:S(2)}) copy-start(bf16[2048]{0:T(1024)(128)(2,1)} %param.27) | copy-start | bytes 12292

commit v4 on v3

--- a/solution.py
+++ b/solution.py
@@ -25,6 +25,9 @@
 PW = QW + 128
 WIN = 64
 CHUNK = 2048
+PARTS = 4
+WIDTH = 2048 // PARTS
+TP_ORDER = (1, 0, 2)
 LOG2E = 1.4426950408889634
 BF16 = jnp.bfloat16
 F32 = jnp.float32
@@ -436,49 +439,58 @@
         context.append((summed / total).astype(BF16))
     context = jnp.concatenate(context, axis=1)
 
-    def over_tp(left, right, width, terms, send, recv):
+    def over_tp(left, right, terms, send, recv):
         copies = []
-        for n in range(4):
-            cols = pl.ds(n * width, width)
+        for n in range(PARTS):
+            cols = pl.ds(n * WIDTH, WIDTH)
             terms[tp, :, cols] = jnp.dot(left, right[:, cols], preferred_element_type=F32).astype(BF16)
-            for d in range(3):
-                ref = terms.at[tp, :, cols]
-                copies.append(
-                    pltpu.make_async_remote_copy(
-                        src_ref=ref, dst_ref=ref, send_sem=send.at[n, d], recv_sem=recv.at[n, d],
-                        device_id=beside[d], device_id_type=MESH,
-                    )
+            ref = terms.at[tp, :, cols]
+            copies.append([
+                pltpu.make_async_remote_copy(
+                    src_ref=ref, dst_ref=ref, send_sem=send.at[n, d], recv_sem=recv.at[n, d],
+                    device_id=beside[d], device_id_type=MESH,
                 )
-                copies[-1].start()
+                for d in TP_ORDER
+            ])
+            for copy in copies[-1]:
+                copy.start()
         return copies
 
-    def summed_terms(terms):
-        total = terms[0].astype(F32)
-        for t in range(1, 4):
-            total = total + terms[t].astype(F32)
+    def summed_terms(first, terms, n):
+        cols = pl.ds(n * WIDTH, WIDTH)
+        total = first
+        for t in range(4):
+            total = total + terms[t, :, cols].astype(F32)
         return total
 
     loads[0].wait()
-    mixes = over_tp(context, wo, 512, mix, ms_sem, mr_sem)
-    for copy in mixes:
-        copy.wait_recv()
-    mid = tok[...].astype(F32) + summed_terms(mix)
-    normed = rms_norm(mid, gain[...])
+    mixes = over_tp(context, wo, mix, ms_sem, mr_sem)
     loads[1].wait()
     loads[2].wait()
-    acts = []
-    for n in range(2):
-        cols = pl.ds(n * 512, 512)
-        gate = jnp.dot(normed, wg[:, cols], preferred_element_type=F32)
-        upper = jnp.dot(normed, wu[:, cols], preferred_element_type=F32)
-        acts.append((gate / (1.0 + jnp.exp(-gate)) * upper).astype(BF16))
-    act = jnp.concatenate(acts, axis=1)
+    mids, squares = [], jnp.zeros((ROWS, 1), F32)
+    gate = jnp.zeros((ROWS, 1024), F32)
+    upper = jnp.zeros((ROWS, 1024), F32)
+    for n in range(PARTS):
+        for copy in mixes[n]:
+            copy.wait_recv()
+        cols = pl.ds(n * WIDTH, WIDTH)
+        mid = summed_terms(tok[:, cols].astype(F32), mix, n)
+        mids.append(mid)
+        squares = squares + jnp.sum(mid * mid, axis=-1, keepdims=True)
+        gains = [gain[pl.ds(n * (WIDTH // 128) + i, 1), :] for i in range(WIDTH // 128)]
+        scaled = (mid * jnp.concatenate(gains, axis=1).astype(F32)).astype(BF16)
+        gate = gate + jnp.dot(scaled, wg[cols, :], preferred_element_type=F32)
+        upper = upper + jnp.dot(scaled, wu[cols, :], preferred_element_type=F32)
+    scale = lax.rsqrt(squares * (1.0 / 2048) + EPS)
+    gate = gate * scale
+    act = (gate / (1.0 + jnp.exp(-gate)) * (upper * scale)).astype(BF16)
     loads[3].wait()
-    downs = over_tp(act, wd, 512, down, ds_sem, dr_sem)
-    for copy in downs:
-        copy.wait_recv()
-    out[...] = mid + summed_terms(down)
-    for copy in [swap] + sends + mixes + downs:
+    downs = over_tp(act, wd, down, ds_sem, dr_sem)
+    for n in range(PARTS):
+        for copy in downs[n]:
+            copy.wait_recv()
+        out[:, pl.ds(n * WIDTH, WIDTH)] = summed_terms(mids[n], down, n)
+    for copy in [swap] + sends + sum(mixes + downs, []):
         copy.wait_send()
 
 

time: 45.8 us -> 44.8 us (0.978)
  Pallas kernels: 44.3 us -> 43.3 us
    pallas_call x1, Pallas kernels: 25.2 us -> 24.2 us  [per_device(): pl.pallas_call(finish_kernel, out_shape=jax.ShapeDtypeStruct((ROWS, 2048)...]
where the time goes in v4:
time: 44.8 us; the launch traced here: 44.7 us
  Pallas kernels  43.3 us (97%)
  between operations  0.73 us (2%)
  local copies, waits for them, and re-layouts  0.68 us (2%)
    pallas_call x1, Pallas kernels, per_device(): pl.pallas_call(finish_kernel, out_shape=jax.ShapeDtypeStruct((ROWS, 2048)...  24.2 us
    pallas_call x1, Pallas kernels, per_device(): pl.pallas_call(project_kernel, out_shape=(jax.ShapeDtypeStruct((REQS, PW)...  15.5 us
    pallas_call x1, Pallas kernels, per_device(): pl.pallas_call(attend_kernel, out_shape=(jax.ShapeDtypeStruct((REQS, PW),...  3.62 us

profile of v4, /device:TPU:0, one launch (start us, length us, event | category | flops | bytes accessed | tf_op | source)
XLA Modules:
  0.0 44.7 jit_solution(17308294015019757261)
XLA Ops:
  0.6 0.0 copy-start.1
  0.6 0.0 copy-start.2
  0.7 15.5 %project.1 = (bf16[512,640]{1,0:T(8,128)(2,1)S(1)}, bf16[16,512]{1,0:T(8,128)(2,1)S(1)}, f32[64,128]{1,0:T(8,128)S(1)}, bf16[4096,512]{1,0:T(8,128)(2,1)S(1)}) custom-call(s32[16]{0:T(128)} %len_h.1, s32[16]{0:T(128)} %pos_h.1, bf16[16,2048]{1,0:T(8,128)(2,1)} %tok.1, bf16[16,128]{1,0:T(8,128)(2,1)} %bitcast.20, f32[8,128]{1,0:T(8,128)} %constant.10.clone.table_h, ...), custom_call_target="tpu_custom_call" | custom-call | tf_op jit(solution)/shard_map/project/pallas_call | solution.py:509
  16.1 0.0 copy-start
  16.1 0.0 copy-start.3
  16.2 0.0 copy-done.1
  16.2 0.0 copy-done.2
  16.2 3.6 %attend.1 = (bf16[512,640]{1,0:T(8,128)(2,1)S(1)}, f32[64,128]{1,0:T(8,128)}) custom-call(s32[1]{0:T(128)} %bitcast.base_s, bf16[512,640]{1,0:T(8,128)(2,1)S(1)} %get-tuple-element.8.qall, s32[4,128]{1,0:T(4,128)S(1)} %bitcast.16, s32[32,128]{1,0:T(8,128)S(1)} %bitcast.15, bf16[4096,512]{1,0:T(8,128)(2,1)S(1)} %get-tuple-element.9.kvd, ...), custom_call_target="tpu_custom_call" | custom-call | tf_op jit(solution)/shard_map/attend/pallas_call | solution.py:543
  19.8 0.0 copy-done
  19.8 0.0 copy-done.3
  19.8 24.2 %finish.1 = f32[16,2048]{1,0:T(8,128)S(1)} custom-call(bf16[512,640]{1,0:T(8,128)(2,1)S(1)} %get-tuple-element.11.pooled, s32[4,128]{1,0:T(4,128)S(1)} %bitcast.17, bf16[16,512]{1,0:T(8,128)(2,1)S(1)} %get-tuple-element.12.qown, f32[64,128]{1,0:T(8,128)S(1)} %get-tuple-element.10.newkv, bf16[16,2048]{1,0:T(8,128)(2,1)S(1)} %copy-done, ...), custom_call_target="tpu_custom_call" | custom-call | tf_op jit(solution)/shard_map/finish/pallas_call | solution.py:561
  44.0 0.7 %copy.21 = f32[16,2048]{1,0:T(8,128)} copy(f32[16,2048]{1,0:T(8,128)S(1)} %finish.1) | data formatting | bytes 262144
Async XLA Ops:
  0.6 15.5 %copy-start.1 = (s32[4096]{0:T(1024)S(1)}, s32[4096]{0:T(1024)}, u32[]{:S(2)}) copy-start(s32[4096]{0:T(1024)} %param.20) | copy-start | bytes 49156
  0.6 15.5 %copy-start.2 = (s32[512]{0:T(512)S(1)}, s32[512]{0:T(512)}, u32[]{:S(2)}) copy-start(s32[512]{0:T(512)} %param.18) | copy-start | bytes 6148
  16.1 3.7 %copy-start = (bf16[16,2048]{1,0:T(8,128)(2,1)S(1)}, bf16[16,2048]{1,0:T(8,128)(2,1)}, u32[]{:S(2)}) copy-start(bf16[16,2048]{1,0:T(8,128)(2,1)} %tok.1) | copy-start | bytes 196612
  16.1 3.7 %copy-start.3 = (bf16[2048]{0:T(1024)(128)(2,1)S(1)}, bf16[2048]{0:T(1024)(128)(2,1)}, u32[]{:S(2)}) copy-start(bf16[2048]{0:T(1024)(128)(2,1)} %param.27) | copy-start | bytes 12292

commit v5 on v4

--- a/solution.py
+++ b/solution.py
@@ -24,7 +24,8 @@
 QW = 512
 PW = QW + 128
 WIN = 64
-CHUNK = 2048
+STEP = 512
+CHUNK = 4096
 PARTS = 4
 WIDTH = 2048 // PARTS
 TP_ORDER = (1, 0, 2)
@@ -91,7 +92,7 @@
     len_h, pos_h, tok_h, gain_h, table_h, wq_h, wk_h, wv_h, pool_h,
     qall, qown_o, newkv_o, kvd,
     len_s, pos_s, tok, gain, table, wq, wk, wv, pool, tmp,
-    s_sem, w_sem, pool_sem, qs_sem, qr_sem, fs_sem, fr_sem,
+    s_sem, w_sem, pool_sem, qs_sem, qr_sem, fs_sem, fr_sem, ds_sem, dr_sem,
 ):
     core, y, z, tp = place()
     chip = y * SIDE + z
@@ -116,7 +117,8 @@
     barrier = pltpu.get_barrier_semaphore()
     sibling = device(chip, 1 - core, tp)
     peers = [sibling] + [device(chip_at(y, z, k), core, tp) for k in range(1, CHIPS)]
-    for peer in peers:
+    across = [device(chip_at(y, z, k), 1 - core, tp) for k in range(1, SIDE)]
+    for peer in peers + across:
         pl.semaphore_signal(barrier, inc=1, device_id=peer, device_id_type=MESH)
 
     for copy in small:
@@ -137,7 +139,7 @@
 
     normed = rms_norm(tok[...].astype(F32), gain[...])
 
-    pl.semaphore_wait(barrier, len(peers))
+    pl.semaphore_wait(barrier, len(peers) + len(across))
     loads[0].wait()
     query = jnp.dot(normed, wq[...], preferred_element_type=F32)
     mine_at = pl.multiple_of(core * HALF + chip * ROWS, ROWS)
@@ -154,8 +156,22 @@
             src_ref=my_rows, dst_ref=my_rows, send_sem=qs_sem.at[k], recv_sem=qr_sem.at[k],
             device_id=peers[k], device_id_type=MESH,
         )
-    far_first = (10, 9, 11, 8, 6, 5, 7, 4, 14, 13, 15, 12, 2, 1, 3)
-    for k in far_first:
+    own_forward = pltpu.make_async_remote_copy(
+        src_ref=my_rows, dst_ref=my_rows, send_sem=fs_sem.at[0], recv_sem=fr_sem.at[0],
+        device_id=sibling, device_id_type=MESH,
+    )
+    directs = [
+        pltpu.make_async_remote_copy(
+            src_ref=my_rows, dst_ref=my_rows, send_sem=ds_sem.at[k], recv_sem=dr_sem.at[k],
+            device_id=across[k - 1], device_id_type=MESH,
+        )
+        for k in range(1, SIDE)
+    ]
+    for k in (10, 9, 11, 8, 6, 5, 7, 4, 14, 13, 15, 12):
+        q_sends[k].start()
+    own_forward.start()
+    for k in (2, 1, 3):
+        directs[k - 1].start()
         q_sends[k].start()
 
     def forward(dy):
@@ -187,12 +203,18 @@
         for j in range(SIDE):
             untangle(4 * i + j)
         for dz in range(SIDE):
-            if dy or dz:
+            if dy:
                 q_sends[dy * SIDE + dz].wait_recv()
-        forwards.append(forward(dy))
-        forwards[-1].start()
+        if dy:
+            forwards.append(forward(dy))
+            forwards[-1].start()
     for copy in forwards:
         copy.wait()
+    own_forward.wait()
+    for copy in directs:
+        copy.wait()
+    for k in range(1, SIDE):
+        q_sends[k].wait_recv()
     for copy in q_sends.values():
         copy.wait_send()
 
@@ -241,7 +263,7 @@
 
     pooled[...] = jnp.zeros_like(pooled)
     slot = lax.broadcasted_iota(jnp.int32, (1, 128), 1)
-    ones = jnp.ones((CHUNK, 128), BF16)
+    ones = jnp.ones((STEP, 128), BF16)
 
     @pl.loop(0, windows)
     def _(w):
@@ -259,22 +281,23 @@
 
         def score(c, peaks):
             start = pl.multiple_of(c * CHUNK, CHUNK)
-            s = [
-                lax.dot_general(
-                    rows[j], kvd[pl.ds(start, CHUNK), pl.ds(2 * j * 128, 128)],
-                    (((1,), (1,)), ((), ())), preferred_element_type=F32,
-                )
-                for j in range(2)
-            ]
             peaks = list(peaks)
-            for i in range(CHUNK // 128):
-                live = mask[pl.ds(c * (CHUNK // 128) + i, 1), :] == 1
-                index = jnp.where(live, slot + (start + i * 128), -REQS * 8192)
-                ok = (index >= first) & (index < last)
+            for n in range(CHUNK // STEP):
+                at_n = pl.multiple_of(start + n * STEP, STEP)
+                oks = []
+                for i in range(STEP // 128):
+                    live = mask[pl.ds(c * (CHUNK // 128) + n * (STEP // 128) + i, 1), :] == 1
+                    index = jnp.where(live, slot + (at_n + i * 128), -REQS * 8192)
+                    oks.append((index >= first) & (index < last))
                 for j in range(2):
-                    found = jnp.where(ok, s[j][:, i * 128:(i + 1) * 128], FLOOR)
-                    scores[j, :, pl.ds(pl.multiple_of(start + i * 128, 128), 128)] = found
-                    peaks[j] = jnp.maximum(peaks[j], found)
+                    s = lax.dot_general(
+                        rows[j], kvd[pl.ds(at_n, STEP), pl.ds(2 * j * 128, 128)],
+                        (((1,), (1,)), ((), ())), preferred_element_type=F32,
+                    )
+                    for i in range(STEP // 128):
+                        found = jnp.where(oks[i], s[:, i * 128:(i + 1) * 128], FLOOR)
+                        scores[j, :, pl.ds(pl.multiple_of(at_n + i * 128, 128), 128)] = found
+                        peaks[j] = jnp.maximum(peaks[j], found)
             return tuple(peaks)
 
         least = jnp.full((2 * WIN, 128), FLOOR, F32)
@@ -284,13 +307,15 @@
 
         def weigh(c, sums):
             start = pl.multiple_of(c * CHUNK, CHUNK)
-            out = []
-            for j in range(2):
-                weight = jnp.exp2((scores[j, :, pl.ds(start, CHUNK)] - peaks[j]) * (SCALE * LOG2E)).astype(BF16)
-                values = kvd[pl.ds(start, CHUNK), pl.ds((2 * j + 1) * 128, 128)]
-                both = jnp.concatenate([values, ones], axis=1)
-                out.append(sums[j] + jnp.dot(weight, both, preferred_element_type=F32))
-            return tuple(out)
+            sums = list(sums)
+            for n in range(CHUNK // STEP):
+                at_n = pl.multiple_of(start + n * STEP, STEP)
+                for j in range(2):
+                    weight = jnp.exp2((scores[j, :, pl.ds(at_n, STEP)] - peaks[j]) * (SCALE * LOG2E)).astype(BF16)
+                    values = kvd[pl.ds(at_n, STEP), pl.ds((2 * j + 1) * 128, 128)]
+                    both = jnp.concatenate([values, ones], axis=1)
+                    sums[j] = sums[j] + jnp.dot(weight, both, preferred_element_type=F32)
+            return tuple(sums)
 
         zero = jnp.zeros((2 * WIN, 256), F32)
         sums = lax.fori_loop(chunk_from, chunk_to, weigh, (zero, zero))
@@ -339,8 +364,8 @@
 
 def finish_kernel(
     pooled, order, qown, newkv, tok, gain, wo_h, wg_h, wu_h, wd_h, out,
-    part, came, comb, rx, mix, down, spread, left_stats, right_stats, wo, wg, wu, wd,
-    w_sem, p_sem, cs_sem, cr_sem, ms_sem, mr_sem, ds_sem, dr_sem,
+    part, came, comb, rx, mix, down, spread, left_stats, right_stats, left_share, right_share, wo, wg, wu, wd,
+    w_sem, ps_sem, pr_sem, cs_sem, cr_sem, ms_sem, mr_sem, ds_sem, dr_sem,
 ):
     core, y, z, tp = place()
     chip = y * SIDE + z
@@ -375,22 +400,25 @@
         return pl.multiple_of(lax.rem(y + dy, SIDE) * 64, 64)
 
     turns = (2, 1, 3, 0)
-    swap = pltpu.make_async_remote_copy(
-        src_ref=part.at[pl.ds(pl.multiple_of(HALF - half, HALF), HALF)], dst_ref=came,
-        send_sem=p_sem.at[0], recv_sem=p_sem.at[1], device_id=sibling, device_id_type=MESH,
-    )
-    swap.start()
-    swap.wait_recv()
-    right_stats[...] = jnp.dot(came[:, pl.ds(QW, 128)], spread[...], preferred_element_type=F32)
+    theirs = pl.ds(pl.multiple_of(HALF - half, HALF), HALF)
+    swaps = [
+        pltpu.make_async_remote_copy(
+            src_ref=part.at[theirs, cols], dst_ref=came.at[:, cols],
+            send_sem=ps_sem.at[i], recv_sem=pr_sem.at[i], device_id=sibling, device_id_type=MESH,
+        )
+        for i, cols in enumerate((pl.ds(QW, 128), pl.ds(0, QW)))
+    ]
+    for swap in swaps:
+        swap.start()
 
     def stat(ref, rows, h):
         totals = ref[rows, pl.ds(QW + h * HEAD_DIM, HEAD_DIM)]
         return jnp.where(totals > 0.0, ref[rows, pl.ds(h * HEAD_DIM, HEAD_DIM)], FLOOR), totals
 
-    sends = []
+    swaps[0].wait_recv()
+    right_stats[...] = jnp.dot(came[:, pl.ds(QW, 128)], spread[...], preferred_element_type=F32)
     for dy in turns:
         rows = pl.ds(rows_of(dy), 64)
-        mine = pl.ds(pl.multiple_of(half + rows_of(dy), 64), 64)
         peaks, totals = [], []
         for h in range(4):
             cols = pl.ds(h * HEAD_DIM, HEAD_DIM)
@@ -400,11 +428,22 @@
             left = total_a * jnp.exp(peak_a - peak)
             right = total_b * jnp.exp(peak_b - peak)
             total = left + right
-            summed = part[mine, cols].astype(F32) * left + came[rows, cols].astype(F32) * right
-            comb[rows, cols] = (summed / jnp.where(total > 0.0, total, 1.0)).astype(BF16)
+            kept = jnp.where(total > 0.0, total, 1.0)
+            left_share[rows, cols] = left / kept
+            right_share[rows, cols] = right / kept
             peaks.append(jnp.where(total > 0.0, peak, 0.0))
             totals.append(total)
         comb[rows, pl.ds(QW, 128)] = stats_of(peaks, totals)
+
+    swaps[1].wait_recv()
+    sends = []
+    for dy in turns:
+        rows = pl.ds(rows_of(dy), 64)
+        mine = pl.ds(pl.multiple_of(half + rows_of(dy), 64), 64)
+        for h in range(4):
+            cols = pl.ds(h * HEAD_DIM, HEAD_DIM)
+            summed = part[mine, cols].astype(F32) * left_share[rows, cols]
+            comb[rows, cols] = (summed + came[rows, cols].astype(F32) * right_share[rows, cols]).astype(BF16)
         for dz in (2, 1, 3, 0):
             k = dy * SIDE + dz
             if k == 0:
@@ -490,7 +529,7 @@
         for copy in downs[n]:
             copy.wait_recv()
         out[:, pl.ds(n * WIDTH, WIDTH)] = summed_terms(mids[n], down, n)
-    for copy in [swap] + sends + sum(mixes + downs, []):
+    for copy in swaps + sends + sum(mixes + downs, []):
         copy.wait_send()
 
 
@@ -527,7 +566,7 @@
             pltpu.VMEM((2048, 256), BF16),
             pltpu.VMEM((4 * SLOTS, HEAD_DIM), BF16),
             pltpu.VMEM((1024, HEAD_DIM), F32),
-            dma((5,)), dma((3,)), dma((4,)), dma((16,)), dma((16,)), dma((4,)), dma((4,)),
+            dma((5,)), dma((3,)), dma((4,)), dma((16,)), dma((16,)), dma((4,)), dma((4,)), dma((4,)), dma((4,)),
         ],
         compiler_params=pltpu.CompilerParams(
             collective_id=0, has_side_effects=True, vmem_limit_bytes=40 << 20
@@ -573,11 +612,13 @@
             pltpu.VMEM((128, 2 * QW), BF16),
             pltpu.VMEM((HALF, 2 * QW), F32),
             pltpu.VMEM((HALF, 2 * QW), F32),
+            pltpu.VMEM((HALF, QW), F32),
+            pltpu.VMEM((HALF, QW), F32),
             pltpu.VMEM((512, 2048), BF16),
             pltpu.VMEM((2048, 1024), BF16),
             pltpu.VMEM((2048, 1024), BF16),
             pltpu.VMEM((1024, 2048), BF16),
-            dma((4,)), dma((2,)), dma((16,)), dma((16,)),
+            dma((4,)), dma((2,)), dma((2,)), dma((16,)), dma((16,)),
             dma((4, 3)), dma((4, 3)), dma((4, 3)), dma((4, 3)),
         ],
         compiler_params=pltpu.CompilerParams(

time: 44.8 us -> 43.9 us (0.980)
  Pallas kernels: 43.3 us -> 42.4 us
    pallas_call x1, Pallas kernels: 3.62 us -> 3.09 us  [per_device(): pl.pallas_call(attend_kernel, out_shape=(jax.ShapeDtypeStruct((REQS, PW),...]
where the time goes in v5:
time: 43.9 us; the launch traced here: 43.8 us
  Pallas kernels  42.4 us (97%)
  between operations  0.73 us (2%)
  local copies, waits for them, and re-layouts  0.68 us (2%)
    pallas_call x1, Pallas kernels, per_device(): pl.pallas_call(finish_kernel, out_shape=jax.ShapeDtypeStruct((ROWS, 2048)...  24 us
    pallas_call x1, Pallas kernels, per_device(): pl.pallas_call(project_kernel, out_shape=(jax.ShapeDtypeStruct((REQS, PW)...  15.3 us
    pallas_call x1, Pallas kernels, per_device(): pl.pallas_call(attend_kernel, out_shape=(jax.ShapeDtypeStruct((REQS, PW),...  3.09 us

profile of v5, /device:TPU:0, one launch (start us, length us, event | category | flops | bytes accessed | tf_op | source)
XLA Modules:
  0.0 43.8 jit_solution(662030429466696096)
XLA Ops:
  0.6 0.0 copy-start.1
  0.6 0.0 copy-start.2
  0.7 15.3 %project.1 = (bf16[512,640]{1,0:T(8,128)(2,1)S(1)}, bf16[16,512]{1,0:T(8,128)(2,1)S(1)}, f32[64,128]{1,0:T(8,128)S(1)}, bf16[4096,512]{1,0:T(8,128)(2,1)S(1)}) custom-call(s32[16]{0:T(128)} %len_h.1, s32[16]{0:T(128)} %pos_h.1, bf16[16,2048]{1,0:T(8,128)(2,1)} %tok.1, bf16[16,128]{1,0:T(8,128)(2,1)} %bitcast.20, f32[8,128]{1,0:T(8,128)} %constant.10.clone.table_h, ...), custom_call_target="tpu_custom_call" | custom-call | tf_op jit(solution)/shard_map/project/pallas_call | solution.py:548
  15.9 0.0 copy-start
  16.0 0.0 copy-start.3
  16.0 0.0 copy-done.1
  16.0 0.0 copy-done.2
  16.0 3.1 %attend.1 = (bf16[512,640]{1,0:T(8,128)(2,1)S(1)}, f32[64,128]{1,0:T(8,128)}) custom-call(s32[1]{0:T(128)} %bitcast.base_s, bf16[512,640]{1,0:T(8,128)(2,1)S(1)} %get-tuple-element.8.qall, s32[4,128]{1,0:T(4,128)S(1)} %bitcast.16, s32[32,128]{1,0:T(8,128)S(1)} %bitcast.15, bf16[4096,512]{1,0:T(8,128)(2,1)S(1)} %get-tuple-element.9.kvd, ...), custom_call_target="tpu_custom_call" | custom-call | tf_op jit(solution)/shard_map/attend/pallas_call | solution.py:582
  19.1 0.0 copy-done
  19.1 0.0 copy-done.3
  19.1 24.0 %finish.1 = f32[16,2048]{1,0:T(8,128)S(1)} custom-call(bf16[512,640]{1,0:T(8,128)(2,1)S(1)} %get-tuple-element.11.pooled, s32[4,128]{1,0:T(4,128)S(1)} %bitcast.17, bf16[16,512]{1,0:T(8,128)(2,1)S(1)} %get-tuple-element.12.qown, f32[64,128]{1,0:T(8,128)S(1)} %get-tuple-element.10.newkv, bf16[16,2048]{1,0:T(8,128)(2,1)S(1)} %copy-done, ...), custom_call_target="tpu_custom_call" | custom-call | tf_op jit(solution)/shard_map/finish/pallas_call | solution.py:600
  43.1 0.7 %copy.21 = f32[16,2048]{1,0:T(8,128)} copy(f32[16,2048]{1,0:T(8,128)S(1)} %finish.1) | data formatting | bytes 262144
Async XLA Ops:
  0.6 15.3 %copy-start.1 = (s32[4096]{0:T(1024)S(1)}, s32[4096]{0:T(1024)}, u32[]{:S(2)}) copy-start(s32[4096]{0:T(1024)} %param.20) | copy-start | bytes 49156
  0.6 15.3 %copy-start.2 = (s32[512]{0:T(512)S(1)}, s32[512]{0:T(512)}, u32[]{:S(2)}) copy-start(s32[512]{0:T(512)} %param.18) | copy-start | bytes 6148
  15.9 3.1 %copy-start = (bf16[16,2048]{1,0:T(8,128)(2,1)S(1)}, bf16[16,2048]{1,0:T(8,128)(2,1)}, u32[]{:S(2)}) copy-start(bf16[16,2048]{1,0:T(8,128)(2,1)} %tok.1) | copy-start | bytes 196612
  16.0 3.1 %copy-start.3 = (bf16[2048]{0:T(1024)(128)(2,1)S(1)}, bf16[2048]{0:T(1024)(128)(2,1)}, u32[]{:S(2)}) copy-start(bf16[2048]{0:T(1024)(128)(2,1)} %param.27) | copy-start | bytes 12292

commit v6 on v5

--- a/solution.py
+++ b/solution.py
@@ -29,6 +29,7 @@
 PARTS = 4
 WIDTH = 2048 // PARTS
 TP_ORDER = (1, 0, 2)
+FAR_FIRST = (10, 9, 11, 6, 14, 8, 2, 5, 7, 13, 15, 4, 12, 1, 3)
 LOG2E = 1.4426950408889634
 BF16 = jnp.bfloat16
 F32 = jnp.float32
@@ -118,7 +119,7 @@
     sibling = device(chip, 1 - core, tp)
     peers = [sibling] + [device(chip_at(y, z, k), core, tp) for k in range(1, CHIPS)]
     across = [device(chip_at(y, z, k), 1 - core, tp) for k in range(1, SIDE)]
-    for peer in peers + across:
+    for peer in [peers[k] for k in FAR_FIRST] + across + [sibling]:
         pl.semaphore_signal(barrier, inc=1, device_id=peer, device_id_type=MESH)
 
     for copy in small:
@@ -373,7 +374,7 @@
     sibling = device(chip, 1 - core, tp)
     peers = [sibling] + [device(chip_at(y, z, k), core, tp) for k in range(1, CHIPS)]
     beside = [device(chip, core, lax.rem(tp + d, 4)) for d in range(1, 4)]
-    for peer in peers + beside:
+    for peer in [peers[k] for k in FAR_FIRST] + [beside[d] for d in TP_ORDER] + [sibling]:
         pl.semaphore_signal(barrier, inc=1, device_id=peer, device_id_type=MESH)
     loads = [
         pltpu.make_async_copy(src, dst, w_sem.at[i])
@@ -429,8 +430,9 @@
             right = total_b * jnp.exp(peak_b - peak)
             total = left + right
             kept = jnp.where(total > 0.0, total, 1.0)
-            left_share[rows, cols] = left / kept
-            right_share[rows, cols] = right / kept
+            inverse = 1.0 / kept
+            left_share[rows, cols] = left * inverse
+            right_share[rows, cols] = right * inverse
             peaks.append(jnp.where(total > 0.0, peak, 0.0))
             totals.append(total)
         comb[rows, pl.ds(QW, 128)] = stats_of(peaks, totals)

time: 43.9 us -> 43.8 us (level)
  no operation moved by 1% of the time
where the time goes in v6:
time: 43.8 us; the launch traced here: 43.7 us
  Pallas kernels  42.3 us (97%)
  between operations  0.73 us (2%)
  local copies, waits for them, and re-layouts  0.68 us (2%)
    pallas_call x1, Pallas kernels, per_device(): pl.pallas_call(finish_kernel, out_shape=jax.ShapeDtypeStruct((ROWS, 2048)...  23.9 us
    pallas_call x1, Pallas kernels, per_device(): pl.pallas_call(project_kernel, out_shape=(jax.ShapeDtypeStruct((REQS, PW)...  15.2 us
    pallas_call x1, Pallas kernels, per_device(): pl.pallas_call(attend_kernel, out_shape=(jax.ShapeDtypeStruct((REQS, PW),...  3.09 us

profile of v6, /device:TPU:0, one launch (start us, length us, event | category | flops | bytes accessed | tf_op | source)
XLA Modules:
  0.0 43.7 jit_solution(9451916985980977277)
XLA Ops:
  0.6 0.0 copy-start.1
  0.6 0.0 copy-start.2
  0.7 15.2 %project.1 = (bf16[512,640]{1,0:T(8,128)(2,1)S(1)}, bf16[16,512]{1,0:T(8,128)(2,1)S(1)}, f32[64,128]{1,0:T(8,128)S(1)}, bf16[4096,512]{1,0:T(8,128)(2,1)S(1)}) custom-call(s32[16]{0:T(128)} %len_h.1, s32[16]{0:T(128)} %pos_h.1, bf16[16,2048]{1,0:T(8,128)(2,1)} %tok.1, bf16[16,128]{1,0:T(8,128)(2,1)} %bitcast.20, f32[8,128]{1,0:T(8,128)} %constant.10.clone.table_h, ...), custom_call_target="tpu_custom_call" | custom-call | tf_op jit(solution)/shard_map/project/pallas_call | solution.py:550
  15.9 0.0 copy-start
  15.9 0.0 copy-start.3
  15.9 0.0 copy-done.1
  15.9 0.0 copy-done.2
  15.9 3.1 %attend.1 = (bf16[512,640]{1,0:T(8,128)(2,1)S(1)}, f32[64,128]{1,0:T(8,128)}) custom-call(s32[1]{0:T(128)} %bitcast.base_s, bf16[512,640]{1,0:T(8,128)(2,1)S(1)} %get-tuple-element.8.qall, s32[4,128]{1,0:T(4,128)S(1)} %bitcast.16, s32[32,128]{1,0:T(8,128)S(1)} %bitcast.15, bf16[4096,512]{1,0:T(8,128)(2,1)S(1)} %get-tuple-element.9.kvd, ...), custom_call_target="tpu_custom_call" | custom-call | tf_op jit(solution)/shard_map/attend/pallas_call | solution.py:584
  19.0 0.0 copy-done
  19.1 0.0 copy-done.3
  19.1 23.9 %finish.1 = f32[16,2048]{1,0:T(8,128)S(1)} custom-call(bf16[512,640]{1,0:T(8,128)(2,1)S(1)} %get-tuple-element.11.pooled, s32[4,128]{1,0:T(4,128)S(1)} %bitcast.17, bf16[16,512]{1,0:T(8,128)(2,1)S(1)} %get-tuple-element.12.qown, f32[64,128]{1,0:T(8,128)S(1)} %get-tuple-element.10.newkv, bf16[16,2048]{1,0:T(8,128)(2,1)S(1)} %copy-done, ...), custom_call_target="tpu_custom_call" | custom-call | tf_op jit(solution)/shard_map/finish/pallas_call | solution.py:602
  43.0 0.7 %copy.21 = f32[16,2048]{1,0:T(8,128)} copy(f32[16,2048]{1,0:T(8,128)S(1)} %finish.1) | data formatting | bytes 262144
Async XLA Ops:
  0.6 15.3 %copy-start.1 = (s32[4096]{0:T(1024)S(1)}, s32[4096]{0:T(1024)}, u32[]{:S(2)}) copy-start(s32[4096]{0:T(1024)} %param.20) | copy-start | bytes 49156
  0.6 15.3 %copy-start.2 = (s32[512]{0:T(512)S(1)}, s32[512]{0:T(512)}, u32[]{:S(2)}) copy-start(s32[512]{0:T(512)} %param.18) | copy-start | bytes 6148
  15.9 3.1 %copy-start = (bf16[16,2048]{1,0:T(8,128)(2,1)S(1)}, bf16[16,2048]{1,0:T(8,128)(2,1)}, u32[]{:S(2)}) copy-start(bf16[16,2048]{1,0:T(8,128)(2,1)} %tok.1) | copy-start | bytes 196612
  15.9 3.1 %copy-start.3 = (bf16[2048]{0:T(1024)(128)(2,1)S(1)}, bf16[2048]{0:T(1024)(128)(2,1)}, u32[]{:S(2)}) copy-start(bf16[2048]{0:T(1024)(128)(2,1)} %param.27) | copy-start | bytes 12292

commit v7 on v5

--- a/solution.py
+++ b/solution.py
@@ -24,7 +24,7 @@
 QW = 512
 PW = QW + 128
 WIN = 64
-STEP = 512
+STEP = 1024
 CHUNK = 4096
 PARTS = 4
 WIDTH = 2048 // PARTS

time: 43.9 us -> 43.9 us (level)
  no operation moved by 1% of the time
where the time goes in v7:
time: 43.9 us; the launch traced here: 43.8 us
  Pallas kernels  42.4 us (97%)
  between operations  0.73 us (2%)
  local copies, waits for them, and re-layouts  0.68 us (2%)
    pallas_call x1, Pallas kernels, per_device(): pl.pallas_call(finish_kernel, out_shape=jax.ShapeDtypeStruct((ROWS, 2048)...  24 us
    pallas_call x1, Pallas kernels, per_device(): pl.pallas_call(project_kernel, out_shape=(jax.ShapeDtypeStruct((REQS, PW)...  15.3 us
    pallas_call x1, Pallas kernels, per_device(): pl.pallas_call(attend_kernel, out_shape=(jax.ShapeDtypeStruct((REQS, PW),...  3.09 us

profile of v7, /device:TPU:0, one launch (start us, length us, event | category | flops | bytes accessed | tf_op | source)
XLA Modules:
  0.0 43.8 jit_solution(17823080643949073460)
XLA Ops:
  0.6 0.0 copy-start.1
  0.6 0.0 copy-start.2
  0.7 15.3 %project.1 = (bf16[512,640]{1,0:T(8,128)(2,1)S(1)}, bf16[16,512]{1,0:T(8,128)(2,1)S(1)}, f32[64,128]{1,0:T(8,128)S(1)}, bf16[4096,512]{1,0:T(8,128)(2,1)S(1)}) custom-call(s32[16]{0:T(128)} %len_h.1, s32[16]{0:T(128)} %pos_h.1, bf16[16,2048]{1,0:T(8,128)(2,1)} %tok.1, bf16[16,128]{1,0:T(8,128)(2,1)} %bitcast.20, f32[8,128]{1,0:T(8,128)} %constant.10.clone.table_h, ...), custom_call_target="tpu_custom_call" | custom-call | tf_op jit(solution)/shard_map/project/pallas_call | solution.py:548
  15.9 0.0 copy-start
  16.0 0.0 copy-start.3
  16.0 0.0 copy-done.1
  16.0 0.0 copy-done.2
  16.0 3.1 %attend.1 = (bf16[512,640]{1,0:T(8,128)(2,1)S(1)}, f32[64,128]{1,0:T(8,128)}) custom-call(s32[1]{0:T(128)} %bitcast.base_s, bf16[512,640]{1,0:T(8,128)(2,1)S(1)} %get-tuple-element.8.qall, s32[4,128]{1,0:T(4,128)S(1)} %bitcast.16, s32[32,128]{1,0:T(8,128)S(1)} %bitcast.15, bf16[4096,512]{1,0:T(8,128)(2,1)S(1)} %get-tuple-element.9.kvd, ...), custom_call_target="tpu_custom_call" | custom-call | tf_op jit(solution)/shard_map/attend/pallas_call | solution.py:582
  19.1 0.0 copy-done
  19.1 0.0 copy-done.3
  19.1 24.0 %finish.1 = f32[16,2048]{1,0:T(8,128)S(1)} custom-call(bf16[512,640]{1,0:T(8,128)(2,1)S(1)} %get-tuple-element.11.pooled, s32[4,128]{1,0:T(4,128)S(1)} %bitcast.17, bf16[16,512]{1,0:T(8,128)(2,1)S(1)} %get-tuple-element.12.qown, f32[64,128]{1,0:T(8,128)S(1)} %get-tuple-element.10.newkv, bf16[16,2048]{1,0:T(8,128)(2,1)S(1)} %copy-done, ...), custom_call_target="tpu_custom_call" | custom-call | tf_op jit(solution)/shard_map/finish/pallas_call | solution.py:600
  43.1 0.7 %copy.21 = f32[16,2048]{1,0:T(8,128)} copy(f32[16,2048]{1,0:T(8,128)S(1)} %finish.1) | data formatting | bytes 262144
Async XLA Ops:
  0.6 15.3 %copy-start.1 = (s32[4096]{0:T(1024)S(1)}, s32[4096]{0:T(1024)}, u32[]{:S(2)}) copy-start(s32[4096]{0:T(1024)} %param.20) | copy-start | bytes 49156
  0.6 15.3 %copy-start.2 = (s32[512]{0:T(512)S(1)}, s32[512]{0:T(512)}, u32[]{:S(2)}) copy-start(s32[512]{0:T(512)} %param.18) | copy-start | bytes 6148
  15.9 3.1 %copy-start = (bf16[16,2048]{1,0:T(8,128)(2,1)S(1)}, bf16[16,2048]{1,0:T(8,128)(2,1)}, u32[]{:S(2)}) copy-start(bf16[16,2048]{1,0:T(8,128)(2,1)} %tok.1) | copy-start | bytes 196612
  16.0 3.1 %copy-start.3 = (bf16[2048]{0:T(1024)(128)(2,1)S(1)}, bf16[2048]{0:T(1024)(128)(2,1)}, u32[]{:S(2)}) copy-start(bf16[2048]{0:T(1024)(128)(2,1)} %param.27) | copy-start | bytes 12292
